TPU v7x, 256 devices: a whole 4x4x8 slice. The times are simulated.
256 devices in a mesh: ctx: 32 (over z, x_hi, core), head: 8 (over x_lo, y).
Axes of the slice: x: 4 (x_hi: 2, x_lo: 2; x = x_hi * 2 + x_lo), y: 4, z: 8, core: 2. Of those that a mesh axis runs over, the one named last changes fastest.
Arguments:
- queries: bfloat16 [16384, 64, 128], P('ctx', 'head'), may hold values from -160 to 160, as said below
- keys: bfloat16 [16384, 8, 128], P('ctx', 'head'), may hold values from -4 to 4
- values: bfloat16 [16384, 8, 128], P('ctx', 'head'), may hold values from -6 to 6
- doc_lengths: int32 [64], replicated, may hold values from 1 to 4096, 16384 in all
Outputs:
- attended: bfloat16 [16384, 8192], P(('ctx', 'head'))
Inputs may be any that keep to these rules, and one draw needn't show every extreme that they name: `queries`: queries of several heads for a few tokens may be large multiples of sums of earlier keys of the same key head. `doc_lengths`: the lengths sum to 16384; the largest is exactly 4096.
All inputs are finite; a program needn't handle non-finite values.
Results may differ from a plain program's by a relative error of at most 0.0033.
Values may be sent and summed in bfloat16 or wider, within the bound.
No kernel may reach another device: no remote copies, remote signals or barrier semaphores. Data moves between devices by JAX's collectives and lax.ppermute only.
A program may use at most 64 MiB of HBM per device.

v0:
```python
import jax
import jax.numpy as jnp
from jax import lax
from jax.sharding import PartitionSpec as P

SPAN = 8


def shifted(value, axis, steps):
    count = lax.axis_size(axis)
    first, last = (max(0, -steps), min(count, count - steps))
    return lax.ppermute(value, axis, [(source, source + steps) for source in range(first, last)])


def doc_index(positions, ends):
    return jnp.sum((ends[None, :] <= positions[:, None]).astype(jnp.int32), axis=1)


def on_device(queries, keys, values, doc_lengths):
    rows, group, hdim = queries.shape
    scale = 1.0 / hdim**0.5
    ends = jnp.cumsum(doc_lengths)
    base = lax.axis_index("ctx") * rows
    qpos = base + jnp.arange(rows, dtype=jnp.int32)
    qdoc = doc_index(qpos, ends)
    own_keys = keys[:, 0, :]
    own_values = values[:, 0, :]

    def update(state, key_block, value_block, first, limit):
        count = key_block.shape[0]
        kpos = first + jnp.arange(count, dtype=jnp.int32)
        kdoc = doc_index(jnp.maximum(kpos, 0), ends)
        mask = (kdoc[None, :] == qdoc[:, None]) & (kpos[None, :] <= qpos[:, None])
        mask = mask & (kpos[None, :] < limit) & (kpos[None, :] >= 0)
        highest, total, acc = state
        score = (
            jnp.einsum("qgd,kd->gqk", queries, key_block, preferred_element_type=jnp.float32)
            * scale
        )
        score = jnp.where(mask[None], score, -1e30)
        newmax = jnp.maximum(highest, jnp.max(score, axis=-1))
        factor = jnp.exp(highest - newmax)
        expo = jnp.exp(score - newmax[..., None])
        total = total * factor + jnp.sum(expo, axis=-1)
        acc = acc * factor.T[:, :, None] + jnp.einsum(
            "gqk,kd->qgd",
            expo.astype(jnp.bfloat16),
            value_block,
            preferred_element_type=jnp.float32,
        )
        return (newmax, total, acc)

    state = (
        jnp.full((group, rows), -1e30, jnp.float32),
        jnp.zeros((group, rows), jnp.float32),
        jnp.zeros((rows, group, hdim), jnp.float32),
    )
    state = update(state, own_keys, own_values, base, base + rows)
    for back in range(1, SPAN + 1):
        arrived = shifted((own_keys, own_values), "ctx", back)
        earlier_key_block = arrived[0]
        earlier_value_block = arrived[1]
        earlier_first = base - back * rows
        last = earlier_first + earlier_key_block.shape[0] - 1
        need = (earlier_first >= 0) & (doc_index(jnp.maximum(last, 0)[None], ends)[0] == qdoc[0])
        state = lax.cond(
            need,
            lambda s: update(s, earlier_key_block, earlier_value_block, earlier_first, base),
            lambda s: s,
            state,
        )
    highest, total, acc = state
    result = (acc / total.T[:, :, None]).reshape(rows, group * hdim).astype(jnp.bfloat16)
    return lax.all_to_all(result, "head", split_axis=0, concat_axis=1, tiled=True)


def solution(mesh):
    placed = (P("ctx", "head", None), P("ctx", "head", None), P("ctx", "head", None), P())
    return jax.shard_map(
        on_device, mesh=mesh, in_specs=placed, out_specs=P(("ctx", "head"), None), check_vma=False
    )
```

profile of v0, /device:TPU:37, one launch (start us, length us, event | category | flops | bytes accessed | tf_op | source)
XLA Modules:
  0.0 165.7 jit_solution(5182854738386249527)
XLA Ops:
  0.0 4.0 %collective-permute-start = (bf16[512,128]{1,0:T(8,128)(2,1)}, bf16[512,128]{1,0:T(8,128)(2,1)S(1)}, u32[]{:S(2)}, u32[]{:S(2)}) collective-permute-start(bf16[512,128]{1,0:T(8,128)(2,1)} %bitcast.217), channel_id=1, source_target_pairs={{0,8},{8,16},{16,24},{24,32},{32,40},{40,48},{48,56},{56,64},{64,7... | collective-permute-start | bytes 393224 | tf_op jit(solution)/shard_map/ppermute | solution.py:12
  4.0 4.7 %collective-permute-start.2 = (bf16[512,128]{1,0:T(8,128)(2,1)}, bf16[512,128]{1,0:T(8,128)(2,1)S(1)}, u32[]{:S(2)}, u32[]{:S(2)}) collective-permute-start(bf16[512,128]{1,0:T(8,128)(2,1)} %bitcast.218), channel_id=1, source_target_pairs={{0,16},{8,24},{16,32},{24,40},{32,48},{40,56},{48,64},{56,72},{64,... | collective-permute-start | bytes 393224 | tf_op jit(solution)/shard_map/ppermute | solution.py:12
  10.9 3.5 %collective-permute-start.3 = (bf16[512,128]{1,0:T(8,128)(2,1)}, bf16[512,128]{1,0:T(8,128)(2,1)S(1)}, u32[]{:S(2)}, u32[]{:S(2)}) collective-permute-start(bf16[512,128]{1,0:T(8,128)(2,1)} %bitcast.46), channel_id=1, source_target_pairs={{0,16},{8,24},{16,32},{24,40},{32,48},{40,56},{48,64},{56,72},{64,... | collective-permute-start | bytes 393224 | tf_op jit(solution)/shard_map/ppermute | solution.py:12
  14.4 5.1 %collective-permute-start.4 = (bf16[512,128]{1,0:T(8,128)(2,1)}, bf16[512,128]{1,0:T(8,128)(2,1)S(1)}, u32[]{:S(2)}, u32[]{:S(2)}) collective-permute-start(bf16[512,128]{1,0:T(8,128)(2,1)} %bitcast.219), channel_id=1, source_target_pairs={{0,24},{8,32},{16,40},{24,48},{32,56},{40,64},{48,72},{56,80},{64,... | collective-permute-start | bytes 393224 | tf_op jit(solution)/shard_map/ppermute | solution.py:12
  22.1 2.9 %fusion.146 = (f32[8,512]{1,0:T(8,128)S(1)}, f32[512,512,8]{1,0,2:T(8,128)S(1)}) fusion(pred[512,512]{0,1:T(8,128)(4,1)S(1)} %and_and_fusion.8, bf16[512,8,128]{2,1,0:T(8,128)(2,1)} %param.20, bf16[512,1,128]{2,0,1:T(8,128)(2,1)} %param.21), kind=kOutput, calls=%fused_computation.188 | convolution fusion | flops 543158272 | bytes 9846784 | tf_op jit(solution)/shard_map/qgd,kd->gqk/dot_general | solution.py:37
  25.1 4.6 %collective-permute-start.5 = (bf16[512,128]{1,0:T(8,128)(2,1)}, bf16[512,128]{1,0:T(8,128)(2,1)S(1)}, u32[]{:S(2)}, u32[]{:S(2)}) collective-permute-start(bf16[512,128]{1,0:T(8,128)(2,1)} %bitcast.46), channel_id=1, source_target_pairs={{0,24},{8,32},{16,40},{24,48},{32,56},{40,64},{48,72},{56,80},{64,... | collective-permute-start | bytes 393224 | tf_op jit(solution)/shard_map/ppermute | solution.py:12
  31.4 2.8 %collective-permute-start.6 = (bf16[512,128]{1,0:T(8,128)(2,1)S(1)}, bf16[512,128]{1,0:T(8,128)(2,1)S(1)}, u32[]{:S(2)}, u32[]{:S(2)}) collective-permute-start(bf16[512,128]{1,0:T(8,128)(2,1)S(1)} %bitcast.220), channel_id=1, source_target_pairs={{0,32},{8,40},{16,48},{24,56},{32,64},{40,72},{48,80},{56,88},{64,... | collective-permute-start | bytes 393224 | tf_op jit(solution)/shard_map/ppermute | solution.py:12
  34.2 2.7 %collective-permute-start.7 = (bf16[512,128]{1,0:T(8,128)(2,1)}, bf16[512,128]{1,0:T(8,128)(2,1)S(1)}, u32[]{:S(2)}, u32[]{:S(2)}) collective-permute-start(bf16[512,128]{1,0:T(8,128)(2,1)} %bitcast.46), channel_id=1, source_target_pairs={{0,32},{8,40},{16,48},{24,56},{32,64},{40,72},{48,80},{56,88},{64,... | collective-permute-start | bytes 393224 | tf_op jit(solution)/shard_map/ppermute | solution.py:12
  36.9 3.3 %collective-permute-start.8 = (bf16[512,128]{1,0:T(8,128)(2,1)S(1)}, bf16[512,128]{1,0:T(8,128)(2,1)S(1)}, u32[]{:S(2)}, u32[]{:S(2)}) collective-permute-start(bf16[512,128]{1,0:T(8,128)(2,1)S(1)} %bitcast.221), channel_id=1, source_target_pairs={{0,40},{8,48},{16,56},{24,64},{32,72},{40,80},{48,88},{56,96},{64,... | collective-permute-start | bytes 393224 | tf_op jit(solution)/shard_map/ppermute | solution.py:12
  42.2 3.8 %collective-permute-start.10 = (bf16[512,128]{1,0:T(8,128)(2,1)S(1)}, bf16[512,128]{1,0:T(8,128)(2,1)S(1)}, u32[]{:S(2)}, u32[]{:S(2)}) collective-permute-start(bf16[512,128]{1,0:T(8,128)(2,1)S(1)} %bitcast.222), channel_id=1, source_target_pairs={{0,48},{8,56},{16,64},{24,72},{32,80},{40,88},{48,96},{56,104},{64... | collective-permute-start | bytes 393224 | tf_op jit(solution)/shard_map/ppermute | solution.py:12
  51.9 11.4 %collective-permute-done.9 = bf16[512,128]{1,0:T(8,128)(2,1)S(1)} collective-permute-done((bf16[512,128]{1,0:T(8,128)(2,1)}, bf16[512,128]{1,0:T(8,128)(2,1)S(1)}, u32[]{:S(2)}, u32[]{:S(2)}) %collective-permute-start.9) | collective-permute-done | bytes 131104 | tf_op jit(solution)/shard_map/ppermute | solution.py:12
  66.0 2.7 %collective-permute-start.15 = (bf16[512,128]{1,0:T(8,128)(2,1)}, bf16[512,128]{1,0:T(8,128)(2,1)}, u32[]{:S(2)}, u32[]{:S(2)}) collective-permute-start(bf16[512,128]{1,0:T(8,128)(2,1)} %bitcast.46), channel_id=1, source_target_pairs={{0,64},{8,72},{16,80},{24,88},{32,96},{40,104},{48,112},{56,120},{... | collective-permute-start | bytes 393224 | tf_op jit(solution)/shard_map/ppermute | solution.py:12
  68.7 3.4 %bitcast_add_fusion.8 = f32[512,8,128]{2,0,1:T(8,128)S(1)} fusion(f32[512,512,8]{1,0,2:T(8,128)S(1)} %get-tuple-element.791, f32[8,512]{1,0:T(8,128)S(1)} %broadcast_maximum_fusion, pred[512,512]{0,1:T(8,128)(4,1)S(1)} %and_and_fusion.8, f32[512,8]{0,1:T(8,128)S(1)} %get-tuple-element.788, bf16[512,1,128]{2,0,1:T(8,128)(2,1)} %param.22), kind=kOutput, calls=%fused_computation.191 | convolution fusion | flops 545783808 | bytes 10911744 | tf_op jit(solution)/shard_map/gqk,kd->qgd/dot_general | solution.py:45
  82.7 9.4 %conditional.8 = ((f32[8,512]{1,0:T(8,128)S(1)}, f32[8,512]{1,0:T(8,128)S(1)}, f32[512,8,128]{2,0,1:T(8,128)S(1)})) conditional(s32[]{:T(128)} %convert_element_type.200, (f32[8,512]{1,0:T(8,128)S(1)}, f32[8,512]{1,0:T(8,128)S(1)}, f32[512,8,128]{2,0,1:T(8,128)S(1)}) %tuple.55, (s32[64]{0:T(128)S(1)}, s32[]{:T(128)}, s32[512]{0:T(512)S(1)}, ...), branch_computations={%region_13.14_spmd, %region_14.18_spmd} | conditional | flops 1099282432 | bytes 32000300 | solution.py:66
  84.0 2.5 %fusion.2 = (f32[8,512]{1,0:T(8,128)S(1)}, f32[512,512,8]{1,0,2:T(8,128)S(1)}) fusion(pred[512,512]{0,1:T(8,128)(4,1)S(1)} %and_and_fusion, bf16[512,8,128]{2,1,0:T(8,128)(2,1)S(1)} %get-tuple-element.631, bf16[512,128]{1,0:T(8,128)(2,1)} %get-tuple-element.233), kind=kOutput, calls=%fused_computation.4 | convolution fusion | flops 543158272 | bytes 9846784 | tf_op jit(solution)/shard_map/cond/branch_1_fun/qgd,kd->gqk/dot_general | solution.py:37
  86.6 3.8 %bitcast_add_fusion = f32[512,8,128]{2,0,1:T(8,128)S(1)} fusion(f32[512,8,128]{2,0,1:T(8,128)S(1)} %get-tuple-element.236, f32[512,512,8]{1,0,2:T(8,128)S(1)} %get-tuple-element.741, f32[8,512]{1,0:T(8,128)S(1)} %get-tuple-element.797, pred[512,512]{0,1:T(8,128)(4,1)S(1)} %and_and_fusion, f32[512,8]{0,1:T(8,128)S(1)} %get-tuple-element.724, ...), kind=kOutput, calls=%fused_computation.7 | convolution fusion | flops 546308096 | bytes 13008896 | tf_op jit(solution)/shard_map/cond/branch_1_fun/gqk,kd->qgd/dot_general | solution.py:45
  92.1 8.0 %conditional.9 = ((f32[8,512]{1,0:T(8,128)S(1)}, f32[8,512]{1,0:T(8,128)S(1)}, f32[512,8,128]{2,0,1:T(8,128)S(1)})) conditional(s32[]{:T(128)} %convert_element_type.198, (f32[8,512]{1,0:T(8,128)S(1)}, f32[8,512]{1,0:T(8,128)S(1)}, f32[512,8,128]{2,0,1:T(8,128)S(1)}) %get-tuple-element.840, (s32[64]{0:T(128)S(1)}, s32[]{:T(128)}, ...), branch_computations={%region_18.19_spmd, %region_19.23_spmd} | conditional | flops 1099282432 | bytes 32524616 | solution.py:66
  92.9 2.5 %fusion.20 = (f32[8,512]{1,0:T(8,128)S(1)}, f32[512,512,8]{1,0,2:T(8,128)S(1)}) fusion(pred[512,512]{0,1:T(8,128)(4,1)S(1)} %and_and_fusion.1, bf16[512,8,128]{2,1,0:T(8,128)(2,1)S(1)} %get-tuple-element.642, bf16[512,128]{1,0:T(8,128)(2,1)} %get-tuple-element.244), kind=kOutput, calls=%fused_computation.27 | convolution fusion | flops 543158272 | bytes 9846784 | tf_op jit(solution)/shard_map/cond/branch_1_fun/qgd,kd->gqk/dot_general | solution.py:37
  95.4 2.9 %bitcast_add_fusion.1 = f32[512,8,128]{2,0,1:T(8,128)S(1)} fusion(f32[512,8,128]{2,0,1:T(8,128)S(1)} %get-tuple-element.247, f32[512,512,8]{1,0,2:T(8,128)S(1)} %get-tuple-element.747, f32[8,512]{1,0:T(8,128)S(1)} %get-tuple-element.803, pred[512,512]{0,1:T(8,128)(4,1)S(1)} %and_and_fusion.1, f32[512,8]{0,1:T(8,128)S(1)} %get-tuple-element.726, ...), kind=kOutput, calls=%fused_computation.30 | convolution fusion | flops 546308096 | bytes 13008896 | tf_op jit(solution)/shard_map/cond/branch_1_fun/gqk,kd->qgd/dot_general | solution.py:45
  100.1 8.1 %conditional.10 = ((f32[8,512]{1,0:T(8,128)S(1)}, f32[8,512]{1,0:T(8,128)S(1)}, f32[512,8,128]{2,0,1:T(8,128)S(1)})) conditional(s32[]{:T(128)} %convert_element_type.196, (f32[8,512]{1,0:T(8,128)S(1)}, f32[8,512]{1,0:T(8,128)S(1)}, f32[512,8,128]{2,0,1:T(8,128)S(1)}) %get-tuple-element.841, (s32[64]{0:T(128)S(1)}, s32[]{:T(128)}, ...), branch_computations={%region_23.24_spmd, %region_24.0_spmd} | conditional | flops 1099282432 | bytes 32524616 | solution.py:66
  103.6 2.9 %bitcast_add_fusion.2 = f32[512,8,128]{2,0,1:T(8,128)S(1)} fusion(f32[512,8,128]{2,0,1:T(8,128)S(1)} %get-tuple-element.258, f32[512,512,8]{1,0,2:T(8,128)S(1)} %get-tuple-element.753, f32[8,512]{1,0:T(8,128)S(1)} %get-tuple-element.809, pred[512,512]{0,1:T(8,128)(4,1)S(1)} %and_and_fusion.2, f32[512,8]{0,1:T(8,128)S(1)} %get-tuple-element.728, ...), kind=kOutput, calls=%fused_computation.53 | convolution fusion | flops 546308096 | bytes 13008896 | tf_op jit(solution)/shard_map/cond/branch_1_fun/gqk,kd->qgd/dot_general | solution.py:45
  108.2 8.0 %conditional.11 = ((f32[8,512]{1,0:T(8,128)S(1)}, f32[8,512]{1,0:T(8,128)S(1)}, f32[512,8,128]{2,0,1:T(8,128)S(1)})) conditional(s32[]{:T(128)} %convert_element_type.194, (f32[8,512]{1,0:T(8,128)S(1)}, f32[8,512]{1,0:T(8,128)S(1)}, f32[512,8,128]{2,0,1:T(8,128)S(1)}) %get-tuple-element.842, (s32[64]{0:T(128)S(1)}, s32[]{:T(128)}, ...), branch_computations={%region_28.29_spmd, %region_29.0_spmd} | conditional | flops 1099282432 | bytes 32524616 | solution.py:66
  111.5 2.9 %bitcast_add_fusion.3 = f32[512,8,128]{2,0,1:T(8,128)S(1)} fusion(f32[512,8,128]{2,0,1:T(8,128)S(1)} %get-tuple-element.269, f32[512,512,8]{1,0,2:T(8,128)S(1)} %get-tuple-element.759, f32[8,512]{1,0:T(8,128)S(1)} %get-tuple-element.815, pred[512,512]{0,1:T(8,128)(4,1)S(1)} %and_and_fusion.3, f32[512,8]{0,1:T(8,128)S(1)} %get-tuple-element.730, ...), kind=kOutput, calls=%fused_computation.76 | convolution fusion | flops 546308096 | bytes 13008896 | tf_op jit(solution)/shard_map/cond/branch_1_fun/gqk,kd->qgd/dot_general | solution.py:45
  116.2 8.2 %conditional.12 = ((f32[8,512]{1,0:T(8,128)S(1)}, f32[8,512]{1,0:T(8,128)S(1)}, f32[512,8,128]{2,0,1:T(8,128)S(1)})) conditional(s32[]{:T(128)} %convert_element_type.192, (f32[8,512]{1,0:T(8,128)S(1)}, f32[8,512]{1,0:T(8,128)S(1)}, f32[512,8,128]{2,0,1:T(8,128)S(1)}) %get-tuple-element.843, (s32[64]{0:T(128)S(1)}, s32[]{:T(128)}, ...), branch_computations={%region_33.34_spmd, %region_34.38_spmd} | conditional | flops 1099282432 | bytes 32524616 | solution.py:66
  119.7 2.9 %bitcast_add_fusion.4 = f32[512,8,128]{2,0,1:T(8,128)S(1)} fusion(f32[512,8,128]{2,0,1:T(8,128)S(1)} %get-tuple-element.280, f32[512,512,8]{1,0,2:T(8,128)S(1)} %get-tuple-element.765, f32[8,512]{1,0:T(8,128)S(1)} %get-tuple-element.821, pred[512,512]{0,1:T(8,128)(4,1)S(1)} %and_and_fusion.4, f32[512,8]{0,1:T(8,128)S(1)} %get-tuple-element.732, ...), kind=kOutput, calls=%fused_computation.99 | convolution fusion | flops 546308096 | bytes 13008896 | tf_op jit(solution)/shard_map/cond/branch_1_fun/gqk,kd->qgd/dot_general | solution.py:45
  124.4 8.8 %conditional.13 = ((f32[8,512]{1,0:T(8,128)S(1)}, f32[8,512]{1,0:T(8,128)S(1)}, f32[512,8,128]{2,0,1:T(8,128)S(1)})) conditional(s32[]{:T(128)} %convert_element_type.190, (f32[8,512]{1,0:T(8,128)S(1)}, f32[8,512]{1,0:T(8,128)S(1)}, f32[512,8,128]{2,0,1:T(8,128)S(1)}) %get-tuple-element.844, (s32[64]{0:T(128)S(1)}, s32[]{:T(128)}, ...), branch_computations={%region_38.39_spmd, %region_39.43_spmd} | conditional | flops 1099282432 | bytes 32000300 | solution.py:66
  125.1 2.5 %fusion.92 = (f32[8,512]{1,0:T(8,128)S(1)}, f32[512,512,8]{1,0,2:T(8,128)S(1)}) fusion(pred[512,512]{0,1:T(8,128)(4,1)S(1)} %and_and_fusion.5, bf16[512,8,128]{2,1,0:T(8,128)(2,1)S(1)} %get-tuple-element.686, bf16[512,128]{1,0:T(8,128)(2,1)} %get-tuple-element.288), kind=kOutput, calls=%fused_computation.119 | convolution fusion | flops 543158272 | bytes 9846784 | tf_op jit(solution)/shard_map/cond/branch_1_fun/qgd,kd->gqk/dot_general | solution.py:37
  127.7 3.8 %bitcast_add_fusion.5 = f32[512,8,128]{2,0,1:T(8,128)S(1)} fusion(f32[512,8,128]{2,0,1:T(8,128)S(1)} %get-tuple-element.291, f32[512,512,8]{1,0,2:T(8,128)S(1)} %get-tuple-element.771, f32[8,512]{1,0:T(8,128)S(1)} %get-tuple-element.827, pred[512,512]{0,1:T(8,128)(4,1)S(1)} %and_and_fusion.5, f32[512,8]{0,1:T(8,128)S(1)} %get-tuple-element.734, ...), kind=kOutput, calls=%fused_computation.122 | convolution fusion | flops 546308096 | bytes 13008896 | tf_op jit(solution)/shard_map/cond/branch_1_fun/gqk,kd->qgd/dot_general | solution.py:45
  133.2 9.1 %conditional.14 = ((f32[8,512]{1,0:T(8,128)S(1)}, f32[8,512]{1,0:T(8,128)S(1)}, f32[512,8,128]{2,0,1:T(8,128)S(1)})) conditional(s32[]{:T(128)} %convert_element_type.188, (f32[8,512]{1,0:T(8,128)S(1)}, f32[8,512]{1,0:T(8,128)S(1)}, f32[512,8,128]{2,0,1:T(8,128)S(1)}) %get-tuple-element.845, (s32[64]{0:T(128)S(1)}, s32[]{:T(128)}, ...), branch_computations={%region_43.44_spmd, %region_44.48_spmd} | conditional | flops 1099282432 | bytes 32000300 | solution.py:66
  134.3 2.5 %fusion.110 = (f32[8,512]{1,0:T(8,128)S(1)}, f32[512,512,8]{1,0,2:T(8,128)S(1)}) fusion(pred[512,512]{0,1:T(8,128)(4,1)S(1)} %and_and_fusion.6, bf16[512,8,128]{2,1,0:T(8,128)(2,1)S(1)} %get-tuple-element.697, bf16[512,128]{1,0:T(8,128)(2,1)} %get-tuple-element.299), kind=kOutput, calls=%fused_computation.142 | convolution fusion | flops 543158272 | bytes 9846784 | tf_op jit(solution)/shard_map/cond/branch_1_fun/qgd,kd->gqk/dot_general | solution.py:37
  136.8 3.8 %bitcast_add_fusion.6 = f32[512,8,128]{2,0,1:T(8,128)S(1)} fusion(f32[512,8,128]{2,0,1:T(8,128)S(1)} %get-tuple-element.302, f32[512,512,8]{1,0,2:T(8,128)S(1)} %get-tuple-element.777, f32[8,512]{1,0:T(8,128)S(1)} %get-tuple-element.833, pred[512,512]{0,1:T(8,128)(4,1)S(1)} %and_and_fusion.6, f32[512,8]{0,1:T(8,128)S(1)} %get-tuple-element.736, ...), kind=kOutput, calls=%fused_computation.145 | convolution fusion | flops 546308096 | bytes 13008896 | tf_op jit(solution)/shard_map/cond/branch_1_fun/gqk,kd->qgd/dot_general | solution.py:45
  144.6 19.6 %all_to_all.16 = bf16[8,64,1024]{2,1,0:T(8,128)(2,1)S(1)} all-to-all(bf16[8,64,1024]{2,1,0:T(8,128)(2,1)S(1)} %convert_element_type.204), channel_id=1, replica_groups=mesh['ctx'=32,'head'=8] {'head'}, dimensions={0} | all-to-all | bytes 2097152 | tf_op jit(solution)/shard_map/all_to_all | solution.py:74
  (129 shorter events, 45.7 us)
Async XLA Ops:
  0.0 25.0 %collective-permute-start = (bf16[512,128]{1,0:T(8,128)(2,1)}, bf16[512,128]{1,0:T(8,128)(2,1)S(1)}, u32[]{:S(2)}, u32[]{:S(2)}) collective-permute-start(bf16[512,128]{1,0:T(8,128)(2,1)} %bitcast.217), channel_id=1, source_target_pairs={{0,8},{8,16},{16,24},{24,32},{32,40},{40,48},{48,56},{56,64},{64,7... | collective-permute-start | bytes 393224 | tf_op jit(solution)/shard_map/ppermute | solution.py:12
  4.0 30.1 %collective-permute-start.2 = (bf16[512,128]{1,0:T(8,128)(2,1)}, bf16[512,128]{1,0:T(8,128)(2,1)S(1)}, u32[]{:S(2)}, u32[]{:S(2)}) collective-permute-start(bf16[512,128]{1,0:T(8,128)(2,1)} %bitcast.218), channel_id=1, source_target_pairs={{0,16},{8,24},{16,32},{24,40},{32,48},{40,56},{48,64},{56,72},{64,... | collective-permute-start | bytes 393224 | tf_op jit(solution)/shard_map/ppermute | solution.py:12
  8.7 22.7 %collective-permute-start.1 = (bf16[512,128]{1,0:T(8,128)(2,1)}, bf16[512,128]{1,0:T(8,128)(2,1)}, u32[]{:S(2)}, u32[]{:S(2)}) collective-permute-start(bf16[512,128]{1,0:T(8,128)(2,1)} %bitcast.46), channel_id=1, source_target_pairs={{0,8},{8,16},{16,24},{24,32},{32,40},{40,48},{48,56},{56,64},{64,7... | collective-permute-start | bytes 393224 | tf_op jit(solution)/shard_map/ppermute | solution.py:12
  10.9 26.0 %collective-permute-start.3 = (bf16[512,128]{1,0:T(8,128)(2,1)}, bf16[512,128]{1,0:T(8,128)(2,1)S(1)}, u32[]{:S(2)}, u32[]{:S(2)}) collective-permute-start(bf16[512,128]{1,0:T(8,128)(2,1)} %bitcast.46), channel_id=1, source_target_pairs={{0,16},{8,24},{16,32},{24,40},{32,48},{40,56},{48,64},{56,72},{64,... | collective-permute-start | bytes 393224 | tf_op jit(solution)/shard_map/ppermute | solution.py:12
  14.4 25.8 %collective-permute-start.4 = (bf16[512,128]{1,0:T(8,128)(2,1)}, bf16[512,128]{1,0:T(8,128)(2,1)S(1)}, u32[]{:S(2)}, u32[]{:S(2)}) collective-permute-start(bf16[512,128]{1,0:T(8,128)(2,1)} %bitcast.219), channel_id=1, source_target_pairs={{0,24},{8,32},{16,40},{24,48},{32,56},{40,64},{48,72},{56,80},{64,... | collective-permute-start | bytes 393224 | tf_op jit(solution)/shard_map/ppermute | solution.py:12
  22.1 9.3 %copy-start.1 = (bf16[512,1,128]{2,0,1:T(8,128)(2,1)S(1)}, bf16[512,1,128]{2,0,1:T(8,128)(2,1)}, u32[]{:S(2)}) copy-start(bf16[512,1,128]{2,0,1:T(8,128)(2,1)} %param.21) | copy-start | bytes 393220
  25.0 4.6 %copy-start.7 = (bf16[512,128]{1,0:T(8,128)(2,1)}, bf16[512,128]{1,0:T(8,128)(2,1)S(1)}, u32[]{:S(2)}) copy-start(bf16[512,128]{1,0:T(8,128)(2,1)S(1)} %collective-permute-done) | copy-start | bytes 393220
  25.1 17.1 %collective-permute-start.5 = (bf16[512,128]{1,0:T(8,128)(2,1)}, bf16[512,128]{1,0:T(8,128)(2,1)S(1)}, u32[]{:S(2)}, u32[]{:S(2)}) collective-permute-start(bf16[512,128]{1,0:T(8,128)(2,1)} %bitcast.46), channel_id=1, source_target_pairs={{0,24},{8,32},{16,40},{24,48},{32,56},{40,64},{48,72},{56,80},{64,... | collective-permute-start | bytes 393224 | tf_op jit(solution)/shard_map/ppermute | solution.py:12
  31.4 51.4 %copy-start = (bf16[512,8,128]{2,1,0:T(8,128)(2,1)S(1)}, bf16[512,8,128]{2,1,0:T(8,128)(2,1)}, u32[]{:S(2)}) copy-start(bf16[512,8,128]{2,1,0:T(8,128)(2,1)} %param.20) | copy-start | bytes 3145732
  31.4 14.6 %collective-permute-start.6 = (bf16[512,128]{1,0:T(8,128)(2,1)S(1)}, bf16[512,128]{1,0:T(8,128)(2,1)S(1)}, u32[]{:S(2)}, u32[]{:S(2)}) collective-permute-start(bf16[512,128]{1,0:T(8,128)(2,1)S(1)} %bitcast.220), channel_id=1, source_target_pairs={{0,32},{8,40},{16,48},{24,56},{32,64},{40,72},{48,80},{56,88},{64,... | collective-permute-start | bytes 393224 | tf_op jit(solution)/shard_map/ppermute | solution.py:12
  34.2 2.7 %copy-start.6 = (bf16[512,128]{1,0:T(8,128)(2,1)}, bf16[512,128]{1,0:T(8,128)(2,1)S(1)}, u32[]{:S(2)}) copy-start(bf16[512,128]{1,0:T(8,128)(2,1)S(1)} %collective-permute-done.2) | copy-start | bytes 393220
  34.2 13.8 %collective-permute-start.7 = (bf16[512,128]{1,0:T(8,128)(2,1)}, bf16[512,128]{1,0:T(8,128)(2,1)S(1)}, u32[]{:S(2)}, u32[]{:S(2)}) collective-permute-start(bf16[512,128]{1,0:T(8,128)(2,1)} %bitcast.46), channel_id=1, source_target_pairs={{0,32},{8,40},{16,48},{24,56},{32,64},{40,72},{48,80},{56,88},{64,... | collective-permute-start | bytes 393224 | tf_op jit(solution)/shard_map/ppermute | solution.py:12
  36.9 5.3 %copy-start.12 = (bf16[512,128]{1,0:T(8,128)(2,1)}, bf16[512,128]{1,0:T(8,128)(2,1)S(1)}, u32[]{:S(2)}) copy-start(bf16[512,128]{1,0:T(8,128)(2,1)S(1)} %collective-permute-done.3) | copy-start | bytes 393220
  36.9 13.0 %collective-permute-start.8 = (bf16[512,128]{1,0:T(8,128)(2,1)S(1)}, bf16[512,128]{1,0:T(8,128)(2,1)S(1)}, u32[]{:S(2)}, u32[]{:S(2)}) collective-permute-start(bf16[512,128]{1,0:T(8,128)(2,1)S(1)} %bitcast.221), channel_id=1, source_target_pairs={{0,40},{8,48},{16,56},{24,64},{32,72},{40,80},{48,88},{56,96},{64,... | collective-permute-start | bytes 393224 | tf_op jit(solution)/shard_map/ppermute | solution.py:12
  40.2 2.0 %copy-start.3 = (bf16[512,128]{1,0:T(8,128)(2,1)}, bf16[512,128]{1,0:T(8,128)(2,1)S(1)}, u32[]{:S(2)}) copy-start(bf16[512,128]{1,0:T(8,128)(2,1)S(1)} %collective-permute-done.4) | copy-start | bytes 393220
  40.2 23.0 %collective-permute-start.9 = (bf16[512,128]{1,0:T(8,128)(2,1)}, bf16[512,128]{1,0:T(8,128)(2,1)S(1)}, u32[]{:S(2)}, u32[]{:S(2)}) collective-permute-start(bf16[512,128]{1,0:T(8,128)(2,1)} %bitcast.46), channel_id=1, source_target_pairs={{0,40},{8,48},{16,56},{24,64},{32,72},{40,80},{48,88},{56,96},{64,... | collective-permute-start | bytes 393224 | tf_op jit(solution)/shard_map/ppermute | solution.py:12
  42.2 26.5 %copy-start.14 = (bf16[512,128]{1,0:T(8,128)(2,1)}, bf16[512,128]{1,0:T(8,128)(2,1)S(1)}, u32[]{:S(2)}) copy-start(bf16[512,128]{1,0:T(8,128)(2,1)S(1)} %collective-permute-done.5) | copy-start | bytes 393220
  42.2 23.8 %collective-permute-start.10 = (bf16[512,128]{1,0:T(8,128)(2,1)S(1)}, bf16[512,128]{1,0:T(8,128)(2,1)S(1)}, u32[]{:S(2)}, u32[]{:S(2)}) collective-permute-start(bf16[512,128]{1,0:T(8,128)(2,1)S(1)} %bitcast.222), channel_id=1, source_target_pairs={{0,48},{8,56},{16,64},{24,72},{32,80},{40,88},{48,96},{56,104},{64... | collective-permute-start | bytes 393224 | tf_op jit(solution)/shard_map/ppermute | solution.py:12
  46.0 22.7 %copy-start.5 = (bf16[512,128]{1,0:T(8,128)(2,1)}, bf16[512,128]{1,0:T(8,128)(2,1)S(1)}, u32[]{:S(2)}) copy-start(bf16[512,128]{1,0:T(8,128)(2,1)S(1)} %collective-permute-done.6) | copy-start | bytes 393220
  46.0 78.3 %collective-permute-start.11 = (bf16[512,128]{1,0:T(8,128)(2,1)}, bf16[512,128]{1,0:T(8,128)(2,1)}, u32[]{:S(2)}, u32[]{:S(2)}) collective-permute-start(bf16[512,128]{1,0:T(8,128)(2,1)} %bitcast.46), channel_id=1, source_target_pairs={{0,48},{8,56},{16,64},{24,72},{32,80},{40,88},{48,96},{56,104},{64... | collective-permute-start | bytes 393224 | tf_op jit(solution)/shard_map/ppermute | solution.py:12
  48.0 20.7 %copy-start.10 = (bf16[512,128]{1,0:T(8,128)(2,1)}, bf16[512,128]{1,0:T(8,128)(2,1)S(1)}, u32[]{:S(2)}) copy-start(bf16[512,128]{1,0:T(8,128)(2,1)S(1)} %collective-permute-done.7) | copy-start | bytes 393220
  48.0 85.2 %collective-permute-start.12 = (bf16[512,128]{1,0:T(8,128)(2,1)S(1)}, bf16[512,128]{1,0:T(8,128)(2,1)}, u32[]{:S(2)}, u32[]{:S(2)}) collective-permute-start(bf16[512,128]{1,0:T(8,128)(2,1)S(1)} %bitcast.223), channel_id=1, source_target_pairs={{0,56},{8,64},{16,72},{24,80},{32,88},{40,96},{48,104},{56,112},{6... | collective-permute-start | bytes 393224 | tf_op jit(solution)/shard_map/ppermute | solution.py:12
  49.9 18.8 %copy-start.4 = (bf16[512,128]{1,0:T(8,128)(2,1)}, bf16[512,128]{1,0:T(8,128)(2,1)S(1)}, u32[]{:S(2)}) copy-start(bf16[512,128]{1,0:T(8,128)(2,1)S(1)} %collective-permute-done.8) | copy-start | bytes 393220
  49.9 83.3 %collective-permute-start.13 = (bf16[512,128]{1,0:T(8,128)(2,1)}, bf16[512,128]{1,0:T(8,128)(2,1)}, u32[]{:S(2)}, u32[]{:S(2)}) collective-permute-start(bf16[512,128]{1,0:T(8,128)(2,1)} %bitcast.46), channel_id=1, source_target_pairs={{0,56},{8,64},{16,72},{24,80},{32,88},{40,96},{48,104},{56,112},{6... | collective-permute-start | bytes 393224 | tf_op jit(solution)/shard_map/ppermute | solution.py:12
  63.3 5.4 %copy-start.8 = (bf16[512,128]{1,0:T(8,128)(2,1)}, bf16[512,128]{1,0:T(8,128)(2,1)S(1)}, u32[]{:S(2)}) copy-start(bf16[512,128]{1,0:T(8,128)(2,1)S(1)} %collective-permute-done.9) | copy-start | bytes 393220
  63.3 79.0 %collective-permute-start.14 = (bf16[512,128]{1,0:T(8,128)(2,1)S(1)}, bf16[512,128]{1,0:T(8,128)(2,1)S(1)}, u32[]{:S(2)}, u32[]{:S(2)}) collective-permute-start(bf16[512,128]{1,0:T(8,128)(2,1)S(1)} %bitcast.224), channel_id=1, source_target_pairs={{0,64},{8,72},{16,80},{24,88},{32,96},{40,104},{48,112},{56,120},{... | collective-permute-start | bytes 393224 | tf_op jit(solution)/shard_map/ppermute | solution.py:12
  66.0 2.7 %copy-start.2 = (bf16[512,128]{1,0:T(8,128)(2,1)}, bf16[512,128]{1,0:T(8,128)(2,1)S(1)}, u32[]{:S(2)}) copy-start(bf16[512,128]{1,0:T(8,128)(2,1)S(1)} %collective-permute-done.10) | copy-start | bytes 393220
  66.0 76.3 %collective-permute-start.15 = (bf16[512,128]{1,0:T(8,128)(2,1)}, bf16[512,128]{1,0:T(8,128)(2,1)}, u32[]{:S(2)}, u32[]{:S(2)}) collective-permute-start(bf16[512,128]{1,0:T(8,128)(2,1)} %bitcast.46), channel_id=1, source_target_pairs={{0,64},{8,72},{16,80},{24,88},{32,96},{40,104},{48,112},{56,120},{... | collective-permute-start | bytes 393224 | tf_op jit(solution)/shard_map/ppermute | solution.py:12
  92.1 3.3 %copy-start.13 = (bf16[512,128]{1,0:T(8,128)(2,1)S(1)}, bf16[512,128]{1,0:T(8,128)(2,1)}, u32[]{:S(2)}) copy-start(bf16[512,128]{1,0:T(8,128)(2,1)} %get-tuple-element.248) | copy-start | bytes 393220 | tf_op jit(solution)/shard_map/cond
  100.3 3.3 %copy-start.15 = (bf16[512,128]{1,0:T(8,128)(2,1)S(1)}, bf16[512,128]{1,0:T(8,128)(2,1)}, u32[]{:S(2)}) copy-start(bf16[512,128]{1,0:T(8,128)(2,1)} %get-tuple-element.259) | copy-start | bytes 393220 | tf_op jit(solution)/shard_map/cond
  108.2 3.3 %copy-start.11 = (bf16[512,128]{1,0:T(8,128)(2,1)S(1)}, bf16[512,128]{1,0:T(8,128)(2,1)}, u32[]{:S(2)}) copy-start(bf16[512,128]{1,0:T(8,128)(2,1)} %get-tuple-element.270) | copy-start | bytes 393220 | tf_op jit(solution)/shard_map/cond
  116.4 3.3 %copy-start.9 = (bf16[512,128]{1,0:T(8,128)(2,1)S(1)}, bf16[512,128]{1,0:T(8,128)(2,1)}, u32[]{:S(2)}) copy-start(bf16[512,128]{1,0:T(8,128)(2,1)} %get-tuple-element.281) | copy-start | bytes 393220 | tf_op jit(solution)/shard_map/cond
where the time goes:
time: 168 us; the launch traced here: 166 us
  starting transfers between devices  48.3 us (29%)
  matrix products  46.5 us (28%)
  other arithmetic  21.7 us (13%)
  blocking collectives  19.6 us (12%)
  waiting for transfers between devices  12.9 us (8%)
  between operations  11.1 us (7%)
  local copies, waits for them, and re-layouts  3.6 us (2%)
  loops' own time  2.06 us (1%)
    ppermute x16, starting transfers between devices, shifted(): lax.ppermute(value, axis, [(source, source + steps) for source in range(f...  48.3 us
    dot_general x8, matrix products, update(): jnp.einsum('gqk,kd->qgd', expo.astype(jnp.bfloat16), value_block, preferr...  26.1 us
    dot_general x8, matrix products, update(): jnp.einsum('qgd,kd->gqk', queries, key_block, preferred_element_type=jnp....  20.4 us
    all_to_all x1, blocking collectives, on_device(): lax.all_to_all(result, 'head', split_axis=0, concat_axis=1, tiled=True)  19.6 us
    reduce_sum x8, other arithmetic, update(): total = total * factor + jnp.sum(expo, axis=-1)  13.9 us
    ppermute x16, waiting for transfers between devices, shifted(): lax.ppermute(value, axis, [(source, source + steps) for source in range(f...  12.9 us
    and x8, other arithmetic, update(): mask = mask & (kpos[None, :] < limit) & (kpos[None, :] >= 0)  5.07 us
  transfers between devices with their start and end apart: 16, of which 2 were waited for; matrix products, arithmetic and copies ran while one was open for 42% of the time, Pallas kernels for 0%

commit v1 on v0

v1 whole, which is shorter than its diff:
```python
import functools

import jax
import jax.numpy as jnp
from jax import lax
from jax.experimental import pallas as pl
from jax.experimental.pallas import tpu as pltpu
from jax.sharding import PartitionSpec as P

NEG = -1e30
NT = (((1,), (1,)), ((), ()))
FAR = ((0, 1), (0, 2), (0, 3), (1, 0), (1, 1), (1, 2), (1, 3), (2, 0), (2, 1), (2, 2), (2, 3))


def kernel(rows, group, tile, sub, factor, me_ref, len_ref, q_ref, *refs):
    count = len(FAR) + 1
    kv_in, out_ref = refs[:count], refs[count]
    kv, m_s, l_s, a_s, start_s, sems = refs[count + 1 :]
    copies = [pltpu.make_async_copy(kv_in[b], kv.at[b], sems.at[b]) for b in range(count)]
    for c in copies:
        c.start()
    me = me_ref[0]
    base = me * rows
    tokens = lax.broadcasted_iota(jnp.int32, (rows, 128), 0)
    ntiles = rows // tile
    start_s[...] = jnp.zeros_like(start_s)

    def doc(d, carry):
        end, lows, highs = carry
        end = end + len_ref[d]
        lows = tuple(jnp.where(end <= base + i * tile, end, lows[i]) for i in range(ntiles))
        highs = tuple(jnp.where(end <= base + i * tile + tile - 1, end, highs[i]) for i in range(ntiles))

        @pl.when(end < base + rows)
        def _():
            @pl.when((end > base) | (end + len_ref[jnp.minimum(d + 1, len_ref.shape[0] - 1)] > base))
            def _():
                start_s[...] = jnp.where(tokens + base >= end, end, start_s[...])

        return end, lows, highs

    zeros = (jnp.int32(0),) * ntiles
    _, lows, highs = lax.fori_loop(0, len_ref.shape[0], doc, (jnp.int32(0), zeros, zeros))
    m_s[...] = jnp.full_like(m_s, NEG)
    l_s[...] = jnp.zeros_like(l_s)
    a_s[...] = jnp.zeros_like(a_s)
    for c in copies:
        c.wait()
    lane = lax.broadcasted_iota(jnp.int32, (1, 128), 1)

    def update(b, first, r, n, k0, keys, masked, causal):
        rs = pl.ds(r, n)
        s = lax.dot_general(q_ref[rs, :], kv[b, k0 : k0 + keys, 0:128], NT, preferred_element_type=jnp.float32)
        parts = [s[:, 128 * j : 128 * j + 128] for j in range(keys // 128)]
        if masked:
            t0, nt = r // group, n // group
            spread = lambda x: jnp.broadcast_to(x[:, None, :], (nt, group, 128)).reshape(n, 128)
            low = spread(start_s[pl.ds(t0, nt), :])
            if causal:
                high = spread(base + t0 + lax.broadcasted_iota(jnp.int32, (nt, 128), 0))
            for j in range(len(parts)):
                pos = first + k0 + 128 * j + lane
                ok = pos >= low
                if causal:
                    ok = ok & (pos <= high)
                parts[j] = jnp.where(ok, parts[j], NEG)
        m = m_s[rs, :]
        top = jnp.max(functools.reduce(jnp.maximum, parts), axis=1, keepdims=True)
        new = jnp.maximum(m, jnp.broadcast_to(top, m.shape))
        parts = [jnp.exp2((x - new) * factor) for x in parts]
        scale = jnp.exp2((m - new) * factor)
        weight = jnp.concatenate([x.astype(jnp.bfloat16) for x in parts], axis=1)
        m_s[rs, :] = new
        l_s[rs, :] = l_s[rs, :] * scale + functools.reduce(jnp.add, parts)
        a_s[rs, :] = a_s[rs, :] * scale + jnp.dot(
            weight, kv[b, k0 : k0 + keys, 128:256], preferred_element_type=jnp.float32
        )

    step = 128
    for t in range(0, rows, step):
        update(0, base, t * group, step * group, 0, t + step, True, True)
    for i in range(ntiles):
        low, high = lows[i], highs[i]

        def block(b, _):
            index = lax.bitwise_xor(me - 4 * (b >> 2), b & 3)
            first = index * rows

            @pl.when((index >= 0) & (index < me) & (first + rows > low))
            def _():
                @pl.when(high <= first)
                def _():
                    for r in range(0, tile * group, sub):
                        update(b, first, i * tile * group + r, sub, 0, rows, False, False)

                @pl.when(high > first)
                def _():
                    for r in range(0, tile * group, sub):
                        update(b, first, i * tile * group + r, sub, 0, rows, True, False)

            return 0

        lax.fori_loop(1, count, block, 0)
    total = jnp.sum(l_s[...], axis=1, keepdims=True)
    out_ref[...] = (a_s[...] / total).astype(out_ref.dtype)


def attend(me, doc_lengths, q, blocks, rows, group, tile=256, sub=2048):
    n, hdim = q.shape
    factor = 1.4426950408889634 / hdim**0.5
    vmem = pl.BlockSpec(memory_space=pltpu.VMEM)
    smem = pl.BlockSpec(memory_space=pltpu.SMEM)
    return pl.pallas_call(
        functools.partial(kernel, rows, group, tile, sub, factor),
        out_shape=jax.ShapeDtypeStruct((n, hdim), jnp.bfloat16),
        in_specs=[smem, smem, vmem] + [pl.BlockSpec(memory_space=pl.ANY)] * len(blocks),
        out_specs=vmem,
        scratch_shapes=[
            pltpu.VMEM((len(blocks), rows, 2 * hdim), jnp.bfloat16),
            pltpu.VMEM((n, hdim), jnp.float32),
            pltpu.VMEM((n, hdim), jnp.float32),
            pltpu.VMEM((n, hdim), jnp.float32),
            pltpu.VMEM((rows, hdim), jnp.int32),
            pltpu.SemaphoreType.DMA((len(blocks),)),
        ],
        compiler_params=pltpu.CompilerParams(vmem_limit_bytes=40 << 20),
        cost_estimate=pl.CostEstimate(flops=20_000_000_000, bytes_accessed=6_000_000, transcendentals=19_000_000),
    )(me, doc_lengths, q, *blocks)


def on_device(queries, keys, values, doc_lengths):
    rows, group, hdim = queries.shape
    count = lax.axis_size("ctx")
    heads = lax.axis_size("head")
    me = lax.axis_index("ctx").reshape(1)
    own = jnp.concatenate([keys[:, 0, :], values[:, 0, :]], axis=1)

    def swap(x, bit):
        return lax.ppermute(x, "ctx", [(i, i ^ bit) for i in range(count)])

    def plane(x):
        return lax.ppermute(x, "ctx", [(i, i + 4) for i in range(count - 4)])

    z1 = plane(own)
    x0 = swap(own, 2)
    c0 = swap(own, 1)
    z2 = plane(z1)
    x1 = swap(z1, 2)
    xc0 = swap(x0, 1)
    c1 = swap(z1, 1)
    x2 = lax.ppermute(z2, "ctx", [(i, i ^ 2) for i in range(count) if i & 2])
    xc1 = swap(x1, 1)
    c2 = swap(z2, 1)
    xc2 = swap(x2, 1)
    blocks = [own, c0, x0, xc0, z1, c1, x1, xc1, z2, c2, x2, xc2]
    out = attend(me, doc_lengths, queries.reshape(rows * group, hdim), blocks, rows, group)
    out = lax.all_to_all(out.reshape(heads, -1, hdim), "head", split_axis=0, concat_axis=0, tiled=True)
    out = out.reshape(heads, rows // heads, group, hdim)
    return jnp.transpose(out, (1, 0, 2, 3)).reshape(rows // heads, heads * group * hdim)


def solution(mesh):
    placed = (P("ctx", "head", None), P("ctx", "head", None), P("ctx", "head", None), P())
    return jax.shard_map(
        on_device, mesh=mesh, in_specs=placed, out_specs=P(("ctx", "head"), None), check_vma=False
    )
```

time: 168 us -> 85.1 us (0.51)
  the two profiles are of different devices: /device:TPU:37 before, /device:TPU:224 now
where the time goes in v1:
time: 85.1 us; the launch traced here: 86.7 us
  Pallas kernels  32.4 us (38%)
  waiting for transfers between devices  24.6 us (29%)
  blocking collectives  16.6 us (20%)
  starting transfers between devices  8.08 us (9%)
  local copies, waits for them, and re-layouts  3.86 us (5%)
  other arithmetic  1 us (1%)
    pallas_call x1, Pallas kernels, attend(): pl.pallas_call(functools.partial(kernel, rows, group, tile, sub, factor),...  32.4 us
    all_to_all x1, blocking collectives, on_device(): lax.all_to_all(out.reshape(heads, -1, hdim), 'head', split_axis=0, concat...  16.6 us
    ppermute x2, waiting for transfers between devices, plane(): return lax.ppermute(x, 'ctx', [(i, i + 4) for i in range(count - 4)])  12.8 us
    ppermute x8, waiting for transfers between devices, swap(): return lax.ppermute(x, 'ctx', [(i, i ^ bit) for i in range(count)])  7.2 us
    ppermute x1, waiting for transfers between devices, on_device(): x2 = lax.ppermute(z2, 'ctx', [(i, i ^ 2) for i in range(count) if i & 2])  4.64 us
    ppermute x8, starting transfers between devices, swap(): return lax.ppermute(x, 'ctx', [(i, i ^ bit) for i in range(count)])  4.23 us
    unnamed x5, local copies, waits for them, and re-layouts  3.58 us
    ppermute x2, starting transfers between devices, plane(): return lax.ppermute(x, 'ctx', [(i, i + 4) for i in range(count - 4)])  2.57 us
  transfers between devices with their start and end apart: 11, of which 6 were waited for; matrix products, arithmetic and copies ran while one was open for 0% of the time, Pallas kernels for 0%

profile of v1, /device:TPU:224, one launch (start us, length us, event | category | flops | bytes accessed | tf_op | source)
XLA Modules:
  0.0 86.7 jit_solution(11977421601978192655)
XLA Ops:
  0.0 1.0 %pad_maximum_fusion.refs_0_ = bf16[512,256]{1,0:T(8,128)(2,1)S(1)} fusion(bf16[512,128]{1,0:T(8,128)(2,1)} %bitcast.16, bf16[512,128]{1,0:T(8,128)(2,1)} %bitcast.17), kind=kLoop, calls=%fused_computation.1 | loop fusion | flops 524288 | bytes 524288 | tf_op jit(solution)/shard_map/concatenate | solution.py:136
  1.0 1.3 %collective-permute-start.3 = (bf16[512,256]{1,0:T(8,128)(2,1)S(1)}, bf16[512,256]{1,0:T(8,128)(2,1)S(1)}, u32[]{:S(2)}, u32[]{:S(2)}) collective-permute-start(bf16[512,256]{1,0:T(8,128)(2,1)S(1)} %pad_maximum_fusion.refs_0_), channel_id=1, source_target_pairs={{0,32},{8,40},{16,48},{24,56},{32,64},{40,72},{48,80},{56,88},{64,... | collective-permute-start | bytes 786440 | tf_op jit(solution)/shard_map/ppermute | solution.py:142
  2.3 8.6 %collective-permute-done.3.refs_4_ = bf16[512,256]{1,0:T(8,128)(2,1)S(1)} collective-permute-done((bf16[512,256]{1,0:T(8,128)(2,1)S(1)}, bf16[512,256]{1,0:T(8,128)(2,1)S(1)}, u32[]{:S(2)}, u32[]{:S(2)}) %collective-permute-start.3) | collective-permute-done | bytes 262176 | tf_op jit(solution)/shard_map/ppermute | solution.py:142
  10.9 1.3 %collective-permute-start.7 = (bf16[512,256]{1,0:T(8,128)(2,1)S(1)}, bf16[512,256]{1,0:T(8,128)(2,1)S(1)}, u32[]{:S(2)}, u32[]{:S(2)}) collective-permute-start(bf16[512,256]{1,0:T(8,128)(2,1)S(1)} %collective-permute-done.3.refs_4_), channel_id=1, source_target_pairs={{0,32},{8,40},{16,48},{24,56},{32,64},{40,72},{48,80},{56,88},{64,... | collective-permute-start | bytes 786440 | tf_op jit(solution)/shard_map/ppermute | solution.py:142
  12.2 3.1 %collective-permute-start.1 = (bf16[512,256]{1,0:T(8,128)(2,1)S(1)}, bf16[512,256]{1,0:T(8,128)(2,1)S(1)}, u32[]{:S(2)}, u32[]{:S(2)}) collective-permute-start(bf16[512,256]{1,0:T(8,128)(2,1)S(1)} %pad_maximum_fusion.refs_0_), channel_id=1, source_target_pairs={{0,16},{8,24},{16,0},{24,8},{32,48},{40,56},{48,32},{56,40},{64,80... | collective-permute-start | bytes 786440 | tf_op jit(solution)/shard_map/ppermute | solution.py:139
  15.3 0.0 collective-permute-start
  15.3 0.5 collective-permute-start.5
  15.8 4.1 %collective-permute-done.7.refs_8_ = bf16[512,256]{1,0:T(8,128)(2,1)S(1)} collective-permute-done((bf16[512,256]{1,0:T(8,128)(2,1)S(1)}, bf16[512,256]{1,0:T(8,128)(2,1)S(1)}, u32[]{:S(2)}, u32[]{:S(2)}) %collective-permute-start.7) | collective-permute-done | bytes 262176 | tf_op jit(solution)/shard_map/ppermute | solution.py:142
  20.0 1.3 %collective-permute-start.9 = (bf16[512,256]{1,0:T(8,128)(2,1)S(1)}, bf16[512,256]{1,0:T(8,128)(2,1)S(1)}, u32[]{:S(2)}, u32[]{:S(2)}) collective-permute-start(bf16[512,256]{1,0:T(8,128)(2,1)S(1)} %collective-permute-done.7.refs_8_), channel_id=1, source_target_pairs={{16,0},{24,8},{48,32},{56,40},{80,64},{88,72},{112,96},{120,104},{... | collective-permute-start | bytes 786440 | tf_op jit(solution)/shard_map/ppermute | solution.py:151
  21.3 0.1 collective-permute-start.4
  21.4 0.7 collective-permute-done.1.refs_2_
  22.1 0.0 collective-permute-start.2
  22.1 0.0 collective-permute-done.refs_1_
  22.1 0.5 collective-permute-start.8
  22.6 5.0 %collective-permute-done.5.refs_6_ = bf16[512,256]{1,0:T(8,128)(2,1)S(1)} collective-permute-done((bf16[512,256]{1,0:T(8,128)(2,1)S(1)}, bf16[512,256]{1,0:T(8,128)(2,1)S(1)}, u32[]{:S(2)}, u32[]{:S(2)}) %collective-permute-start.5) | collective-permute-done | bytes 262176 | tf_op jit(solution)/shard_map/ppermute | solution.py:139
  27.6 0.0 collective-permute-start.6
  27.6 4.6 %collective-permute-done.9.refs_10_ = bf16[512,256]{1,0:T(8,128)(2,1)S(1)} collective-permute-done((bf16[512,256]{1,0:T(8,128)(2,1)S(1)}, bf16[512,256]{1,0:T(8,128)(2,1)S(1)}, u32[]{:S(2)}, u32[]{:S(2)}) %collective-permute-start.9) | collective-permute-done | bytes 262176 | tf_op jit(solution)/shard_map/ppermute | solution.py:151
  32.2 0.0 collective-permute-start.10
  32.2 0.0 collective-permute-done.4.refs_5_
  32.2 0.0 collective-permute-done.2.refs_3_
  32.2 0.0 collective-permute-done.8.refs_9_
  32.3 0.0 collective-permute-done.6.refs_7_
  32.3 1.5 %collective-permute-done.10.refs_11_ = bf16[512,256]{1,0:T(8,128)(2,1)S(1)} collective-permute-done((bf16[512,256]{1,0:T(8,128)(2,1)S(1)}, bf16[512,256]{1,0:T(8,128)(2,1)S(1)}, u32[]{:S(2)}, u32[]{:S(2)}) %collective-permute-start.10) | collective-permute-done | bytes 262176 | tf_op jit(solution)/shard_map/ppermute | solution.py:139
  33.8 0.0 copy-start.1
  33.8 0.7 copy-done.1
  34.4 0.0 copy-start
  34.4 1.2 %copy-done = bf16[512,8,128]{2,1,0:T(8,128)(2,1)S(1)} copy-done((bf16[512,8,128]{2,1,0:T(8,128)(2,1)S(1)}, bf16[512,8,128]{2,1,0:T(8,128)(2,1)}, u32[]{:S(2)}) %copy-start) | copy-done | bytes 1048600
  35.6 32.4 %shard_map.46 = bf16[4096,128]{1,0:T(8,128)(2,1)S(1)} custom-call(s32[1]{0:T(128)} %bitcast.me_ref, s32[64]{0:T(128)S(1)} %copy-done.1, bf16[4096,128]{1,0:T(8,128)(2,1)S(1)} %bitcast.13, bf16[512,256]{1,0:T(8,128)(2,1)S(1)} %pad_maximum_fusion.refs_0_, bf16[512,256]{1,0:T(8,128)(2,1)S(1)} %collective-permute-done.refs_1_, ...), custom_call_target="tpu_custom_call" | custom-call | flops 20000000000 | bytes 6000000 | tf_op jit(solution)/shard_map/pallas_call | solution.py:113
  68.1 16.6 %all_to_all.5 = bf16[8,512,128]{2,1,0:T(8,128)(2,1)S(1)} all-to-all(bf16[8,512,128]{2,1,0:T(8,128)(2,1)S(1)} %bitcast.12), channel_id=1, replica_groups=mesh['ctx'=32,'head'=8] {'head'}, dimensions={0} | all-to-all | bytes 2097152 | tf_op jit(solution)/shard_map/all_to_all | solution.py:157
  84.7 0.3 copy.5
  85.0 1.7 %copy.8 = bf16[8,8,64,128]{3,1,2,0:T(8,128)(2,1)} copy(bf16[8,8,64,128]{3,2,1,0:T(8,128)(2,1)S(1)} %bitcast.15) | data formatting | bytes 2097152
Async XLA Ops:
  1.0 9.9 %collective-permute-start.3 = (bf16[512,256]{1,0:T(8,128)(2,1)S(1)}, bf16[512,256]{1,0:T(8,128)(2,1)S(1)}, u32[]{:S(2)}, u32[]{:S(2)}) collective-permute-start(bf16[512,256]{1,0:T(8,128)(2,1)S(1)} %pad_maximum_fusion.refs_0_), channel_id=1, source_target_pairs={{0,32},{8,40},{16,48},{24,56},{32,64},{40,72},{48,80},{56,88},{64,... | collective-permute-start | bytes 786440 | tf_op jit(solution)/shard_map/ppermute | solution.py:142
  10.9 9.1 %collective-permute-start.7 = (bf16[512,256]{1,0:T(8,128)(2,1)S(1)}, bf16[512,256]{1,0:T(8,128)(2,1)S(1)}, u32[]{:S(2)}, u32[]{:S(2)}) collective-permute-start(bf16[512,256]{1,0:T(8,128)(2,1)S(1)} %collective-permute-done.3.refs_4_), channel_id=1, source_target_pairs={{0,32},{8,40},{16,48},{24,56},{32,64},{40,72},{48,80},{56,88},{64,... | collective-permute-start | bytes 786440 | tf_op jit(solution)/shard_map/ppermute | solution.py:142
  12.2 9.9 %collective-permute-start.1 = (bf16[512,256]{1,0:T(8,128)(2,1)S(1)}, bf16[512,256]{1,0:T(8,128)(2,1)S(1)}, u32[]{:S(2)}, u32[]{:S(2)}) collective-permute-start(bf16[512,256]{1,0:T(8,128)(2,1)S(1)} %pad_maximum_fusion.refs_0_), channel_id=1, source_target_pairs={{0,16},{8,24},{16,0},{24,8},{32,48},{40,56},{48,32},{56,40},{64,80... | collective-permute-start | bytes 786440 | tf_op jit(solution)/shard_map/ppermute | solution.py:139
  15.3 6.8 %collective-permute-start = (bf16[512,256]{1,0:T(8,128)(2,1)S(1)}, bf16[512,256]{1,0:T(8,128)(2,1)S(1)}, u32[]{:S(2)}, u32[]{:S(2)}) collective-permute-start(bf16[512,256]{1,0:T(8,128)(2,1)S(1)} %pad_maximum_fusion.refs_0_), channel_id=1, source_target_pairs={{0,8},{8,0},{16,24},{24,16},{32,40},{40,32},{48,56},{56,48},{64,72... | collective-permute-start | bytes 786440 | tf_op jit(solution)/shard_map/ppermute | solution.py:139
  15.3 12.2 %collective-permute-start.5 = (bf16[512,256]{1,0:T(8,128)(2,1)S(1)}, bf16[512,256]{1,0:T(8,128)(2,1)S(1)}, u32[]{:S(2)}, u32[]{:S(2)}) collective-permute-start(bf16[512,256]{1,0:T(8,128)(2,1)S(1)} %collective-permute-done.3.refs_4_), channel_id=1, source_target_pairs={{0,16},{8,24},{16,0},{24,8},{32,48},{40,56},{48,32},{56,40},{64,80... | collective-permute-start | bytes 786440 | tf_op jit(solution)/shard_map/ppermute | solution.py:139
  20.0 12.2 %collective-permute-start.9 = (bf16[512,256]{1,0:T(8,128)(2,1)S(1)}, bf16[512,256]{1,0:T(8,128)(2,1)S(1)}, u32[]{:S(2)}, u32[]{:S(2)}) collective-permute-start(bf16[512,256]{1,0:T(8,128)(2,1)S(1)} %collective-permute-done.7.refs_8_), channel_id=1, source_target_pairs={{16,0},{24,8},{48,32},{56,40},{80,64},{88,72},{112,96},{120,104},{... | collective-permute-start | bytes 786440 | tf_op jit(solution)/shard_map/ppermute | solution.py:151
  21.3 10.9 %collective-permute-start.4 = (bf16[512,256]{1,0:T(8,128)(2,1)S(1)}, bf16[512,256]{1,0:T(8,128)(2,1)S(1)}, u32[]{:S(2)}, u32[]{:S(2)}) collective-permute-start(bf16[512,256]{1,0:T(8,128)(2,1)S(1)} %collective-permute-done.3.refs_4_), channel_id=1, source_target_pairs={{0,8},{8,0},{16,24},{24,16},{32,40},{40,32},{48,56},{56,48},{64,72... | collective-permute-start | bytes 786440 | tf_op jit(solution)/shard_map/ppermute | solution.py:139
  22.1 10.1 %collective-permute-start.2 = (bf16[512,256]{1,0:T(8,128)(2,1)S(1)}, bf16[512,256]{1,0:T(8,128)(2,1)S(1)}, u32[]{:S(2)}, u32[]{:S(2)}) collective-permute-start(bf16[512,256]{1,0:T(8,128)(2,1)S(1)} %collective-permute-done.1.refs_2_), channel_id=1, source_target_pairs={{0,8},{8,0},{16,24},{24,16},{32,40},{40,32},{48,56},{56,48},{64,72... | collective-permute-start | bytes 786440 | tf_op jit(solution)/shard_map/ppermute | solution.py:139
  22.1 10.1 %collective-permute-start.8 = (bf16[512,256]{1,0:T(8,128)(2,1)S(1)}, bf16[512,256]{1,0:T(8,128)(2,1)S(1)}, u32[]{:S(2)}, u32[]{:S(2)}) collective-permute-start(bf16[512,256]{1,0:T(8,128)(2,1)S(1)} %collective-permute-done.7.refs_8_), channel_id=1, source_target_pairs={{0,8},{8,0},{16,24},{24,16},{32,40},{40,32},{48,56},{56,48},{64,72... | collective-permute-start | bytes 786440 | tf_op jit(solution)/shard_map/ppermute | solution.py:139
  27.6 4.7 %collective-permute-start.6 = (bf16[512,256]{1,0:T(8,128)(2,1)S(1)}, bf16[512,256]{1,0:T(8,128)(2,1)S(1)}, u32[]{:S(2)}, u32[]{:S(2)}) collective-permute-start(bf16[512,256]{1,0:T(8,128)(2,1)S(1)} %collective-permute-done.5.refs_6_), channel_id=1, source_target_pairs={{0,8},{8,0},{16,24},{24,16},{32,40},{40,32},{48,56},{56,48},{64,72... | collective-permute-start | bytes 786440 | tf_op jit(solution)/shard_map/ppermute | solution.py:139
  32.2 1.5 %collective-permute-start.10 = (bf16[512,256]{1,0:T(8,128)(2,1)S(1)}, bf16[512,256]{1,0:T(8,128)(2,1)S(1)}, u32[]{:S(2)}, u32[]{:S(2)}) collective-permute-start(bf16[512,256]{1,0:T(8,128)(2,1)S(1)} %collective-permute-done.9.refs_10_), channel_id=1, source_target_pairs={{0,8},{8,0},{16,24},{24,16},{32,40},{40,32},{48,56},{56,48},{64,72... | collective-permute-start | bytes 786440 | tf_op jit(solution)/shard_map/ppermute | solution.py:139
  33.8 0.7 copy-start.1
  34.4 1.2 %copy-start = (bf16[512,8,128]{2,1,0:T(8,128)(2,1)S(1)}, bf16[512,8,128]{2,1,0:T(8,128)(2,1)}, u32[]{:S(2)}) copy-start(bf16[512,8,128]{2,1,0:T(8,128)(2,1)} %param.4) | copy-start | bytes 3145732

commit v2 on v1

--- a/solution.py
+++ b/solution.py
@@ -9,16 +9,19 @@
 
 NEG = -1e30
 NT = (((1,), (1,)), ((), ()))
-FAR = ((0, 1), (0, 2), (0, 3), (1, 0), (1, 1), (1, 2), (1, 3), (2, 0), (2, 1), (2, 2), (2, 3))
 
 
-def kernel(rows, group, tile, sub, factor, me_ref, len_ref, q_ref, *refs):
-    count = len(FAR) + 1
-    kv_in, out_ref = refs[:count], refs[count]
-    kv, m_s, l_s, a_s, start_s, sems = refs[count + 1 :]
+def kernel(first_stage, last_stage, origin, rows, group, tile, sub, factor, me_ref, len_ref, q_ref, *refs):
+    refs, sems = refs[:-1], refs[-1]
+    refs, kv, start_s = refs[:-2], refs[-2], refs[-1]
+    count = kv.shape[0]
+    kv_in, refs = refs[:count], refs[count:]
     copies = [pltpu.make_async_copy(kv_in[b], kv.at[b], sems.at[b]) for b in range(count)]
     for c in copies:
         c.start()
+    if not first_stage:
+        refs = refs[3:]
+    m_s, l_s, a_s = refs[-3:]
     me = me_ref[0]
     base = me * rows
     tokens = lax.broadcasted_iota(jnp.int32, (rows, 128), 0)
@@ -33,7 +36,7 @@
 
         @pl.when(end < base + rows)
         def _():
-            @pl.when((end > base) | (end + len_ref[jnp.minimum(d + 1, len_ref.shape[0] - 1)] > base))
+            @pl.when(end + len_ref[jnp.minimum(d + 1, len_ref.shape[0] - 1)] > base)
             def _():
                 start_s[...] = jnp.where(tokens + base >= end, end, start_s[...])
 
@@ -41,9 +44,10 @@
 
     zeros = (jnp.int32(0),) * ntiles
     _, lows, highs = lax.fori_loop(0, len_ref.shape[0], doc, (jnp.int32(0), zeros, zeros))
-    m_s[...] = jnp.full_like(m_s, NEG)
-    l_s[...] = jnp.zeros_like(l_s)
-    a_s[...] = jnp.zeros_like(a_s)
+    if first_stage:
+        m_s[...] = jnp.full_like(m_s, NEG)
+        l_s[...] = jnp.zeros_like(l_s)
+        a_s[...] = jnp.zeros_like(a_s)
     for c in copies:
         c.wait()
     lane = lax.broadcasted_iota(jnp.int32, (1, 128), 1)
@@ -76,14 +80,15 @@
             weight, kv[b, k0 : k0 + keys, 128:256], preferred_element_type=jnp.float32
         )
 
-    step = 128
-    for t in range(0, rows, step):
-        update(0, base, t * group, step * group, 0, t + step, True, True)
+    if first_stage:
+        step = 128
+        for t in range(0, rows, step):
+            update(0, base, t * group, step * group, 0, t + step, True, True)
     for i in range(ntiles):
         low, high = lows[i], highs[i]
 
         def block(b, _):
-            index = lax.bitwise_xor(me - 4 * (b >> 2), b & 3)
+            index = lax.bitwise_xor(me - 4 * ((origin + b) >> 2), (origin + b) & 3)
             first = index * rows
 
             @pl.when((index >= 0) & (index < me) & (first + rows > low))
@@ -100,32 +105,34 @@
 
             return 0
 
-        lax.fori_loop(1, count, block, 0)
-    total = jnp.sum(l_s[...], axis=1, keepdims=True)
-    out_ref[...] = (a_s[...] / total).astype(out_ref.dtype)
+        lax.fori_loop(1 if first_stage else 0, count, block, 0)
+    if last_stage:
+        total = jnp.sum(l_s[...], axis=1, keepdims=True)
+        refs[0][...] = (a_s[...] / total).astype(refs[0].dtype)
 
 
-def attend(me, doc_lengths, q, blocks, rows, group, tile=256, sub=2048):
+def stage(me, doc_lengths, q, blocks, origin, state, last, rows, group, tile=256, sub=2048):
     n, hdim = q.shape
     factor = 1.4426950408889634 / hdim**0.5
     vmem = pl.BlockSpec(memory_space=pltpu.VMEM)
     smem = pl.BlockSpec(memory_space=pltpu.SMEM)
-    return pl.pallas_call(
-        functools.partial(kernel, rows, group, tile, sub, factor),
-        out_shape=jax.ShapeDtypeStruct((n, hdim), jnp.bfloat16),
-        in_specs=[smem, smem, vmem] + [pl.BlockSpec(memory_space=pl.ANY)] * len(blocks),
-        out_specs=vmem,
-        scratch_shapes=[
-            pltpu.VMEM((len(blocks), rows, 2 * hdim), jnp.bfloat16),
-            pltpu.VMEM((n, hdim), jnp.float32),
-            pltpu.VMEM((n, hdim), jnp.float32),
-            pltpu.VMEM((n, hdim), jnp.float32),
-            pltpu.VMEM((rows, hdim), jnp.int32),
-            pltpu.SemaphoreType.DMA((len(blocks),)),
-        ],
-        compiler_params=pltpu.CompilerParams(vmem_limit_bytes=40 << 20),
-        cost_estimate=pl.CostEstimate(flops=20_000_000_000, bytes_accessed=6_000_000, transcendentals=19_000_000),
-    )(me, doc_lengths, q, *blocks)
+    held = [pltpu.VMEM((n, hdim), jnp.float32)] * 3
+    scratch = [pltpu.VMEM((len(blocks), rows, 2 * hdim), jnp.bfloat16), pltpu.VMEM((rows, hdim), jnp.int32)]
+    outs = [pltpu.VMEM((n, hdim), jnp.bfloat16)] if last else []
+    nin = 3 + len(blocks)
+    result = pl.pallas_call(
+        functools.partial(kernel, state is None, last, origin, rows, group, tile, sub, factor),
+        out_shape=outs + held,
+        in_specs=[smem, smem, vmem] + [pl.BlockSpec(memory_space=pl.ANY)] * len(blocks) + [vmem] * (0 if state is None else 3),
+        out_specs=[vmem] * (len(outs) + 3),
+        input_output_aliases={} if state is None else {nin + i: len(outs) + i for i in range(3)},
+        scratch_shapes=scratch + [pltpu.SemaphoreType.DMA((len(blocks),))],
+        compiler_params=pltpu.CompilerParams(vmem_limit_bytes=28 << 20),
+        cost_estimate=pl.CostEstimate(
+            flops=2_000_000_000 * len(blocks), bytes_accessed=300_000 * len(blocks), transcendentals=2_000_000 * len(blocks)
+        ),
+    )(me, doc_lengths, q, *blocks, *(state or ()))
+    return result[0] if last else tuple(result)
 
 
 def on_device(queries, keys, values, doc_lengths):
@@ -141,19 +148,25 @@
     def plane(x):
         return lax.ppermute(x, "ctx", [(i, i + 4) for i in range(count - 4)])
 
+    q = pltpu.with_memory_space_constraint(queries.reshape(rows * group, hdim), pltpu.VMEM)
     z1 = plane(own)
     x0 = swap(own, 2)
     c0 = swap(own, 1)
+    state = stage(me, doc_lengths, q, [own, c0], 0, None, False, rows, group)
+    z1, x0, state = lax.optimization_barrier((z1, x0, state))
     z2 = plane(z1)
     x1 = swap(z1, 2)
     xc0 = swap(x0, 1)
     c1 = swap(z1, 1)
+    state = stage(me, doc_lengths, q, [x0, xc0, z1, c1], 2, state, False, rows, group)
+    z2, x1, state = lax.optimization_barrier((z2, x1, state))
     x2 = lax.ppermute(z2, "ctx", [(i, i ^ 2) for i in range(count) if i & 2])
     xc1 = swap(x1, 1)
     c2 = swap(z2, 1)
+    state = stage(me, doc_lengths, q, [x1, xc1, z2, c2], 6, state, False, rows, group)
+    x2, state = lax.optimization_barrier((x2, state))
     xc2 = swap(x2, 1)
-    blocks = [own, c0, x0, xc0, z1, c1, x1, xc1, z2, c2, x2, xc2]
-    out = attend(me, doc_lengths, queries.reshape(rows * group, hdim), blocks, rows, group)
+    out = stage(me, doc_lengths, q, [x2, xc2], 10, state, True, rows, group)
     out = lax.all_to_all(out.reshape(heads, -1, hdim), "head", split_axis=0, concat_axis=0, tiled=True)
     out = out.reshape(heads, rows // heads, group, hdim)
     return jnp.transpose(out, (1, 0, 2, 3)).reshape(rows // heads, heads * group * hdim)

time: 85.1 us -> 77 us (0.905)
  the two profiles are of different devices: /device:TPU:224 before, /device:TPU:64 now
where the time goes in v2:
time: 77 us; the launch traced here: 75.6 us
  Pallas kernels  25.2 us (33%)
  blocking collectives  20.2 us (26%)
  starting transfers between devices  17 us (22%)
  waiting for transfers between devices  8.2 us (11%)
  local copies, waits for them, and re-layouts  3.86 us (5%)
  other arithmetic  1 us (1%)
    pallas_call x4, Pallas kernels, stage(): pl.pallas_call(functools.partial(kernel, state is None, last, origin, row...  25.2 us
    all_to_all x1, blocking collectives, on_device(): lax.all_to_all(out.reshape(heads, -1, hdim), 'head', split_axis=0, concat...  20.2 us
    ppermute x2, starting transfers between devices, plane(): return lax.ppermute(x, 'ctx', [(i, i + 4) for i in range(count - 4)])  7.76 us
    ppermute x8, starting transfers between devices, swap(): return lax.ppermute(x, 'ctx', [(i, i ^ bit) for i in range(count)])  7.74 us
    ppermute x1, waiting for transfers between devices, on_device(): x2 = lax.ppermute(z2, 'ctx', [(i, i ^ 2) for i in range(count) if i & 2])  6.64 us
    unnamed x5, local copies, waits for them, and re-layouts  3.57 us
    ppermute x8, waiting for transfers between devices, swap(): return lax.ppermute(x, 'ctx', [(i, i ^ bit) for i in range(count)])  1.55 us
  transfers between devices with their start and end apart: 11, of which 2 were waited for; matrix products, arithmetic and copies ran while one was open for 0% of the time, Pallas kernels for 30%

profile of v2, /device:TPU:64, one launch (start us, length us, event | category | flops | bytes accessed | tf_op | source)
XLA Modules:
  0.0 75.6 jit_solution(7549561157929336224)
XLA Ops:
  0.0 1.0 %pad_maximum_fusion.refs_0_ = bf16[512,256]{1,0:T(8,128)(2,1)S(1)} fusion(bf16[512,128]{1,0:T(8,128)(2,1)} %bitcast.19, bf16[512,128]{1,0:T(8,128)(2,1)} %bitcast.20), kind=kLoop, calls=%fused_computation.1 | loop fusion | flops 524288 | bytes 524288 | tf_op jit(solution)/shard_map/concatenate | solution.py:143
  1.0 0.1 collective-permute-start.2
  1.1 3.1 %collective-permute-start.1 = (bf16[512,256]{1,0:T(8,128)(2,1)S(1)}, bf16[512,256]{1,0:T(8,128)(2,1)S(1)}, u32[]{:S(2)}, u32[]{:S(2)}) collective-permute-start(bf16[512,256]{1,0:T(8,128)(2,1)S(1)} %pad_maximum_fusion.refs_0_), channel_id=1, source_target_pairs={{0,16},{8,24},{16,0},{24,8},{32,48},{40,56},{48,32},{56,40},{64,80... | collective-permute-start | bytes 786440 | tf_op jit(solution)/shard_map/ppermute | solution.py:146
  4.2 3.8 %collective-permute-start = (bf16[512,256]{1,0:T(8,128)(2,1)S(1)}, bf16[512,256]{1,0:T(8,128)(2,1)S(1)}, u32[]{:S(2)}, u32[]{:S(2)}) collective-permute-start(bf16[512,256]{1,0:T(8,128)(2,1)S(1)} %pad_maximum_fusion.refs_0_), channel_id=1, source_target_pairs={{0,32},{8,40},{16,48},{24,56},{32,64},{40,72},{48,80},{56,88},{64,... | collective-permute-start | bytes 786440 | tf_op jit(solution)/shard_map/ppermute | solution.py:149
  8.0 0.0 collective-permute-done.2.refs_1_
  8.0 0.0 copy-start
  8.1 1.2 %copy-done = bf16[512,8,128]{2,1,0:T(8,128)(2,1)S(1)} copy-done((bf16[512,8,128]{2,1,0:T(8,128)(2,1)S(1)}, bf16[512,8,128]{2,1,0:T(8,128)(2,1)}, u32[]{:S(2)}) %copy-start) | copy-done | bytes 1048600
  9.3 0.7 copy-done.1
  9.9 5.4 %shard_map.46 = (f32[4096,128]{1,0:T(8,128)S(1)}, f32[4096,128]{1,0:T(8,128)S(1)}, f32[4096,128]{1,0:T(8,128)S(1)}) custom-call(s32[1]{0:T(128)} %bitcast.me_ref, s32[64]{0:T(128)S(1)} %copy-done.1, bf16[4096,128]{1,0:T(8,128)(2,1)S(1)} %bitcast.13, bf16[512,256]{1,0:T(8,128)(2,1)S(1)} %pad_maximum_fusion.refs_0_, ...), custom_call_target="tpu_custom_call" | custom-call | flops 4000000000 | bytes 600000 | tf_op jit(solution)/shard_map/pallas_call | solution.py:123
  15.3 0.0 collective-permute-done.1.refs_0_
  15.3 0.0 collective-permute-done.refs_2_
  15.3 3.1 %collective-permute-start.5 = (bf16[512,256]{1,0:T(8,128)(2,1)S(1)}, bf16[512,256]{1,0:T(8,128)(2,1)S(1)}, u32[]{:S(2)}, u32[]{:S(2)}) collective-permute-start(bf16[512,256]{1,0:T(8,128)(2,1)S(1)} %collective-permute-done.1.refs_0_), channel_id=1, source_target_pairs={{0,8},{8,0},{16,24},{24,16},{32,40},{40,32},{48,56},{56,48},{64,72... | collective-permute-start | bytes 786440 | tf_op jit(solution)/shard_map/ppermute | solution.py:146
  18.5 0.3 collective-permute-start.6
  18.8 0.5 collective-permute-start.4
  19.3 3.9 %collective-permute-start.3 = (bf16[512,256]{1,0:T(8,128)(2,1)S(1)}, bf16[512,256]{1,0:T(8,128)(2,1)S(1)}, u32[]{:S(2)}, u32[]{:S(2)}) collective-permute-start(bf16[512,256]{1,0:T(8,128)(2,1)S(1)} %collective-permute-done.refs_2_), channel_id=1, source_target_pairs={{0,32},{8,40},{16,48},{24,56},{32,64},{40,72},{48,80},{56,88},{64,... | collective-permute-start | bytes 786440 | tf_op jit(solution)/shard_map/ppermute | solution.py:149
  23.2 0.0 collective-permute-done.5.refs_1_
  23.2 0.0 collective-permute-done.6.refs_3_
  23.3 8.9 %shard_map.47 = (f32[4096,128]{1,0:T(8,128)S(1)}, f32[4096,128]{1,0:T(8,128)S(1)}, f32[4096,128]{1,0:T(8,128)S(1)}) custom-call(s32[1]{0:T(128)} %bitcast.me_ref, s32[64]{0:T(128)S(1)} %copy-done.1, bf16[4096,128]{1,0:T(8,128)(2,1)S(1)} %bitcast.14, ...), custom_call_target="tpu_custom_call", output_to_operand_aliasing={{0}: (7, {}), {1}: (8, {}), {2}: (9, {})} | custom-call | flops 8000000000 | bytes 1200000 | tf_op jit(solution)/shard_map/pallas_call | solution.py:123
  32.2 0.0 collective-permute-done.4.refs_0_
  32.2 0.0 collective-permute-done.3.refs_2_
  32.2 0.1 collective-permute-start.8
  32.3 0.5 collective-permute-start.9
  32.8 1.5 %collective-permute-start.7 = (bf16[512,256]{1,0:T(8,128)(2,1)S(1)}, bf16[512,256]{1,0:T(8,128)(2,1)S(1)}, u32[]{:S(2)}, u32[]{:S(2)}) collective-permute-start(bf16[512,256]{1,0:T(8,128)(2,1)S(1)} %collective-permute-done.3.refs_2_), channel_id=1, source_target_pairs={{16,0},{24,8},{48,32},{56,40},{80,64},{88,72},{112,96},{120,104},{... | collective-permute-start | bytes 786440 | tf_op jit(solution)/shard_map/ppermute | solution.py:163
  34.3 0.0 collective-permute-done.9.refs_3_
  34.3 8.4 %shard_map.48 = (f32[4096,128]{1,0:T(8,128)S(1)}, f32[4096,128]{1,0:T(8,128)S(1)}, f32[4096,128]{1,0:T(8,128)S(1)}) custom-call(s32[1]{0:T(128)} %bitcast.me_ref, s32[64]{0:T(128)S(1)} %copy-done.1, bf16[4096,128]{1,0:T(8,128)(2,1)S(1)} %bitcast.15, ...), custom_call_target="tpu_custom_call", output_to_operand_aliasing={{0}: (7, {}), {1}: (8, {}), {2}: (9, {})} | custom-call | flops 8000000000 | bytes 1200000 | tf_op jit(solution)/shard_map/pallas_call | solution.py:123
  42.7 6.6 %collective-permute-done.7.refs_0_ = bf16[512,256]{1,0:T(8,128)(2,1)S(1)} collective-permute-done((bf16[512,256]{1,0:T(8,128)(2,1)S(1)}, bf16[512,256]{1,0:T(8,128)(2,1)S(1)}, u32[]{:S(2)}, u32[]{:S(2)}) %collective-permute-start.7) | collective-permute-done | bytes 262176 | tf_op jit(solution)/shard_map/ppermute | solution.py:163
  49.3 0.0 collective-permute-start.10
  49.3 1.5 %collective-permute-done.10.refs_1_ = bf16[512,256]{1,0:T(8,128)(2,1)S(1)} collective-permute-done((bf16[512,256]{1,0:T(8,128)(2,1)S(1)}, bf16[512,256]{1,0:T(8,128)(2,1)S(1)}, u32[]{:S(2)}, u32[]{:S(2)}) %collective-permute-start.10) | collective-permute-done | bytes 262176 | tf_op jit(solution)/shard_map/ppermute | solution.py:146
  50.9 2.5 %shard_map.49 = (bf16[4096,128]{1,0:T(8,128)(2,1)S(1)}, f32[4096,128]{1,0:T(8,128)S(1)}, f32[4096,128]{1,0:T(8,128)S(1)}, f32[4096,128]{1,0:T(8,128)S(1)}) custom-call(s32[1]{0:T(128)} %bitcast.me_ref, s32[64]{0:T(128)S(1)} %copy-done.1, bf16[4096,128]{1,0:T(8,128)(2,1)S(1)} %bitcast.16, ...), custom_call_target="tpu_custom_call", output_to_operand_aliasing={{1}: (5, {}), {2}: (6, {}), {3}: (7, {})} | custom-call | flops 4000000000 | bytes 600000 | tf_op jit(solution)/shard_map/pallas_call | solution.py:123
  53.4 20.2 %all_to_all.5 = bf16[8,512,128]{2,1,0:T(8,128)(2,1)S(1)} all-to-all(bf16[8,512,128]{2,1,0:T(8,128)(2,1)S(1)} %bitcast.12), channel_id=1, replica_groups=mesh['ctx'=32,'head'=8] {'head'}, dimensions={0} | all-to-all | bytes 2097152 | tf_op jit(solution)/shard_map/all_to_all | solution.py:170
  73.6 0.3 copy.14
  73.9 1.7 %copy.17 = bf16[8,8,64,128]{3,1,2,0:T(8,128)(2,1)} copy(bf16[8,8,64,128]{3,2,1,0:T(8,128)(2,1)S(1)} %bitcast.18) | data formatting | bytes 2097152
  (2 shorter events, 0.0 us)
Async XLA Ops:
  1.0 7.0 %collective-permute-start.2 = (bf16[512,256]{1,0:T(8,128)(2,1)S(1)}, bf16[512,256]{1,0:T(8,128)(2,1)S(1)}, u32[]{:S(2)}, u32[]{:S(2)}) collective-permute-start(bf16[512,256]{1,0:T(8,128)(2,1)S(1)} %pad_maximum_fusion.refs_0_), channel_id=1, source_target_pairs={{0,8},{8,0},{16,24},{24,16},{32,40},{40,32},{48,56},{56,48},{64,72... | collective-permute-start | bytes 786440 | tf_op jit(solution)/shard_map/ppermute | solution.py:146
  1.1 14.2 %collective-permute-start.1 = (bf16[512,256]{1,0:T(8,128)(2,1)S(1)}, bf16[512,256]{1,0:T(8,128)(2,1)S(1)}, u32[]{:S(2)}, u32[]{:S(2)}) collective-permute-start(bf16[512,256]{1,0:T(8,128)(2,1)S(1)} %pad_maximum_fusion.refs_0_), channel_id=1, source_target_pairs={{0,16},{8,24},{16,0},{24,8},{32,48},{40,56},{48,32},{56,40},{64,80... | collective-permute-start | bytes 786440 | tf_op jit(solution)/shard_map/ppermute | solution.py:146
  4.2 11.1 %collective-permute-start = (bf16[512,256]{1,0:T(8,128)(2,1)S(1)}, bf16[512,256]{1,0:T(8,128)(2,1)S(1)}, u32[]{:S(2)}, u32[]{:S(2)}) collective-permute-start(bf16[512,256]{1,0:T(8,128)(2,1)S(1)} %pad_maximum_fusion.refs_0_), channel_id=1, source_target_pairs={{0,32},{8,40},{16,48},{24,56},{32,64},{40,72},{48,80},{56,88},{64,... | collective-permute-start | bytes 786440 | tf_op jit(solution)/shard_map/ppermute | solution.py:149
  8.0 1.2 %copy-start = (bf16[512,8,128]{2,1,0:T(8,128)(2,1)S(1)}, bf16[512,8,128]{2,1,0:T(8,128)(2,1)}, u32[]{:S(2)}) copy-start(bf16[512,8,128]{2,1,0:T(8,128)(2,1)} %param.4) | copy-start | bytes 3145732
  9.3 0.7 copy-start.1
  15.3 7.9 %collective-permute-start.5 = (bf16[512,256]{1,0:T(8,128)(2,1)S(1)}, bf16[512,256]{1,0:T(8,128)(2,1)S(1)}, u32[]{:S(2)}, u32[]{:S(2)}) collective-permute-start(bf16[512,256]{1,0:T(8,128)(2,1)S(1)} %collective-permute-done.1.refs_0_), channel_id=1, source_target_pairs={{0,8},{8,0},{16,24},{24,16},{32,40},{40,32},{48,56},{56,48},{64,72... | collective-permute-start | bytes 786440 | tf_op jit(solution)/shard_map/ppermute | solution.py:146
  18.5 4.8 %collective-permute-start.6 = (bf16[512,256]{1,0:T(8,128)(2,1)S(1)}, bf16[512,256]{1,0:T(8,128)(2,1)S(1)}, u32[]{:S(2)}, u32[]{:S(2)}) collective-permute-start(bf16[512,256]{1,0:T(8,128)(2,1)S(1)} %collective-permute-done.refs_2_), channel_id=1, source_target_pairs={{0,8},{8,0},{16,24},{24,16},{32,40},{40,32},{48,56},{56,48},{64,72... | collective-permute-start | bytes 786440 | tf_op jit(solution)/shard_map/ppermute | solution.py:146
  18.8 13.4 %collective-permute-start.4 = (bf16[512,256]{1,0:T(8,128)(2,1)S(1)}, bf16[512,256]{1,0:T(8,128)(2,1)S(1)}, u32[]{:S(2)}, u32[]{:S(2)}) collective-permute-start(bf16[512,256]{1,0:T(8,128)(2,1)S(1)} %collective-permute-done.refs_2_), channel_id=1, source_target_pairs={{0,16},{8,24},{16,0},{24,8},{32,48},{40,56},{48,32},{56,40},{64,80... | collective-permute-start | bytes 786440 | tf_op jit(solution)/shard_map/ppermute | solution.py:146
  19.3 12.9 %collective-permute-start.3 = (bf16[512,256]{1,0:T(8,128)(2,1)S(1)}, bf16[512,256]{1,0:T(8,128)(2,1)S(1)}, u32[]{:S(2)}, u32[]{:S(2)}) collective-permute-start(bf16[512,256]{1,0:T(8,128)(2,1)S(1)} %collective-permute-done.refs_2_), channel_id=1, source_target_pairs={{0,32},{8,40},{16,48},{24,56},{32,64},{40,72},{48,80},{56,88},{64,... | collective-permute-start | bytes 786440 | tf_op jit(solution)/shard_map/ppermute | solution.py:149
  32.2 2.1 %collective-permute-start.8 = (bf16[512,256]{1,0:T(8,128)(2,1)S(1)}, bf16[512,256]{1,0:T(8,128)(2,1)S(1)}, u32[]{:S(2)}, u32[]{:S(2)}) collective-permute-start(bf16[512,256]{1,0:T(8,128)(2,1)S(1)} %collective-permute-done.4.refs_0_), channel_id=1, source_target_pairs={{0,8},{8,0},{16,24},{24,16},{32,40},{40,32},{48,56},{56,48},{64,72... | collective-permute-start | bytes 786440 | tf_op jit(solution)/shard_map/ppermute | solution.py:146
  32.3 2.0 %collective-permute-start.9 = (bf16[512,256]{1,0:T(8,128)(2,1)S(1)}, bf16[512,256]{1,0:T(8,128)(2,1)S(1)}, u32[]{:S(2)}, u32[]{:S(2)}) collective-permute-start(bf16[512,256]{1,0:T(8,128)(2,1)S(1)} %collective-permute-done.3.refs_2_), channel_id=1, source_target_pairs={{0,8},{8,0},{16,24},{24,16},{32,40},{40,32},{48,56},{56,48},{64,72... | collective-permute-start | bytes 786440 | tf_op jit(solution)/shard_map/ppermute | solution.py:146
  32.8 16.5 %collective-permute-start.7 = (bf16[512,256]{1,0:T(8,128)(2,1)S(1)}, bf16[512,256]{1,0:T(8,128)(2,1)S(1)}, u32[]{:S(2)}, u32[]{:S(2)}) collective-permute-start(bf16[512,256]{1,0:T(8,128)(2,1)S(1)} %collective-permute-done.3.refs_2_), channel_id=1, source_target_pairs={{16,0},{24,8},{48,32},{56,40},{80,64},{88,72},{112,96},{120,104},{... | collective-permute-start | bytes 786440 | tf_op jit(solution)/shard_map/ppermute | solution.py:163
  49.3 1.5 %collective-permute-start.10 = (bf16[512,256]{1,0:T(8,128)(2,1)S(1)}, bf16[512,256]{1,0:T(8,128)(2,1)S(1)}, u32[]{:S(2)}, u32[]{:S(2)}) collective-permute-start(bf16[512,256]{1,0:T(8,128)(2,1)S(1)} %collective-permute-done.7.refs_0_), channel_id=1, source_target_pairs={{0,8},{8,0},{16,24},{24,16},{32,40},{40,32},{48,56},{56,48},{64,72... | collective-permute-start | bytes 786440 | tf_op jit(solution)/shard_map/ppermute | solution.py:146

commit v3 on v1

v3 whole, which is shorter than its diff:
```python
import functools

import jax
import jax.numpy as jnp
from jax import lax
from jax.experimental import pallas as pl
from jax.experimental.pallas import tpu as pltpu
from jax.sharding import PartitionSpec as P

NEG = -1e30
NT = (((1,), (1,)), ((), ()))
HALF = 256
GROUP = 256
VMEM = pl.BlockSpec(memory_space=pltpu.VMEM)
SMEM = pl.BlockSpec(memory_space=pltpu.SMEM)


def first_doc(base, len_ref, visit):
    def doc(d, carry):
        end, low, high = carry
        length = len_ref[d]
        visit(end, length)
        here = (end <= base) & (end + length > base)
        return end + length, jnp.where(here, end, low), jnp.where(here, end + length, high)

    _, low, high = lax.fori_loop(0, len_ref.shape[0], doc, (jnp.int32(0),) * 3)
    return low, high


def own_kernel(rows, group, factor, me_ref, len_ref, q_hbm, kv_ref, qx_ref, m_ref, la_ref, q_s, start_s, sem):
    n, hdim = q_s.shape
    copy = pltpu.make_async_copy(q_hbm, q_s, sem)
    copy.start()
    base = me_ref[0] * rows
    tokens = base + lax.broadcasted_iota(jnp.int32, (rows, hdim), 0)
    start_s[...] = jnp.zeros_like(start_s)

    def visit(start, length):
        @pl.when((start < base + rows) & (start + length > base))
        def _():
            start_s[...] = jnp.where(tokens >= start, start, start_s[...])

    _, high = first_doc(base, len_ref, visit)
    lane = lax.broadcasted_iota(jnp.int32, (1, hdim), 1)
    token = base + lax.broadcasted_iota(jnp.int32, (n, hdim), 0) // group
    flag = (lane == 0) | ((lane == 1) & (token >= high))
    qx_ref[:, hdim : 2 * hdim] = jnp.where(flag, 1.0, 0.0).astype(jnp.bfloat16)
    copy.wait()
    qx_ref[:, 0:hdim] = q_s[...]
    step = 128
    for t in range(0, rows, step):
        keys, many = t + step, step * group
        rs = pl.ds(t * group, many)
        s = lax.dot_general(q_s[rs, :], kv_ref[0:keys, 0:hdim], NT, preferred_element_type=jnp.float32)
        spread = lambda x: jnp.broadcast_to(x[:, None, :], (step, group, hdim)).reshape(many, hdim)
        low = spread(start_s[pl.ds(t, step), :])
        now = spread(base + t + lax.broadcasted_iota(jnp.int32, (step, hdim), 0))
        parts = []
        for j in range(0, keys, hdim):
            pos = base + j + lane
            ok = pos >= low
            if j + hdim > t:
                ok = ok & (pos <= now)
            parts.append(jnp.where(ok, s[:, j : j + hdim], NEG))
        top = jnp.max(functools.reduce(jnp.maximum, parts), axis=1, keepdims=True)
        top = jnp.broadcast_to(top, (many, hdim))
        parts = [jnp.exp2((x - top) * factor) for x in parts]
        total = jnp.sum(functools.reduce(jnp.add, parts), axis=1, keepdims=True)
        weight = jnp.concatenate([x.astype(jnp.bfloat16) for x in parts], axis=1)
        m_ref[rs, :] = top
        la_ref[rs, 0:hdim] = jnp.broadcast_to(total, (many, hdim))
        la_ref[rs, hdim : 2 * hdim] = jnp.dot(
            weight, kv_ref[0:keys, hdim : 2 * hdim], preferred_element_type=jnp.float32
        )


def later_kernel(origin, count, last, rows, factor, me_ref, len_ref, qx_ref, *refs):
    blocks, refs = refs[:count], refs[count + 2 :]
    out_ref = refs[0] if last else None
    m_ref, la_ref, kx, vx = refs[-4:]
    n = qx_ref.shape[0]
    hdim = qx_ref.shape[1] // 2
    me = me_ref[0]
    low, _ = first_doc(me * rows, len_ref, lambda start, length: None)
    groups = n // GROUP
    steps = groups * (rows // HALF)

    def index_of(code):
        return lax.bitwise_xor(me - 4 * (code >> 2), code & 3)

    def needed(index):
        return (index >= 0) & (index < me) & (index * rows + rows > low)

    lane = lax.broadcasted_iota(jnp.int32, (rows, hdim), 1)
    place = lax.broadcasted_iota(jnp.int32, (rows, hdim), 0)
    for b in range(count):
        index = index_of(jnp.int32(origin + b))

        @pl.when(needed(index))
        def _():
            early = jnp.where(place + index * rows >= low, 0.0, NEG)
            kx[b, :, 0:hdim] = blocks[b][:, 0:hdim]
            kx[b, :, hdim : 2 * hdim] = jnp.where(lane == 0, early, jnp.where(lane == 1, NEG, 0.0)).astype(jnp.bfloat16)
            vx[b, :, 0:hdim] = jnp.ones((rows, hdim), jnp.bfloat16)
            vx[b, :, hdim : 2 * hdim] = blocks[b][:, hdim : 2 * hdim]

    def attend(b, score, mixed):
        def soften(s, g):
            rs = pl.ds(g * GROUP, GROUP)
            m = m_ref[rs, :]
            s0, s1 = s[:, 0:hdim], s[:, hdim : 2 * hdim]
            top = jnp.max(jnp.maximum(s0, s1), axis=1, keepdims=True)
            new = jnp.maximum(m, jnp.broadcast_to(top, m.shape))
            weight = jnp.concatenate([jnp.exp2((x - new) * factor).astype(jnp.bfloat16) for x in (s0, s1)], axis=1)
            m_ref[rs, :] = new
            return weight, jnp.exp2((m - new) * factor)

        def flush(o, g, scale):
            rs = pl.ds(g * GROUP, GROUP)
            for j in (0, hdim):
                la_ref[rs, j : j + hdim] = la_ref[rs, j : j + hdim] * scale + o[:, j : j + hdim]

        def multiply(acc, lhs, step):
            fresh = step // groups if step % groups == 0 else None
            pltpu.matmul_acc_lhs(acc, lhs, load_staged_rhs=fresh)

        for h in range(rows // HALF):
            pltpu.matmul_push_rhs(kx[b, h * HALF : (h + 1) * HALF, :], h, 0, transpose=True)
            pltpu.matmul_push_rhs(vx[b, h * HALF : (h + 1) * HALF, :], h, 1)
        done = []
        for t in range(-1, steps + 2):
            if t + 1 < steps:
                multiply(score[(t + 1) % 2], qx_ref[pl.ds((t + 1) % groups * GROUP, GROUP), :], t + 1)
            if 0 <= t < steps:
                done.append(soften(pltpu.matmul_pop(score[t % 2]), t % groups))
            if 1 <= t < steps + 1:
                multiply(mixed[(t - 1) % 2], done[t - 1][0], t - 1)
            if 2 <= t:
                flush(pltpu.matmul_pop(mixed[(t - 2) % 2]), (t - 2) % groups, done[t - 2][1])

    def run(s0, s1, p0, p1):
        @pl.loop(0, count)
        def _(b):
            @pl.when(needed(index_of(origin + b)))
            def _():
                attend(b, (s0, s1), (p0, p1))

    score = pltpu.ACC(mxu_id=0)((GROUP, 2 * hdim), jnp.float32)
    mixed = pltpu.ACC(mxu_id=1)((GROUP, 2 * hdim), jnp.float32)
    pl.run_scoped(run, score, score, mixed, mixed)
    if last:
        out_ref[...] = (la_ref[:, hdim : 2 * hdim] / la_ref[:, 0:hdim]).astype(out_ref.dtype)


def own_stage(me, doc_lengths, q, kv, rows, group, factor):
    n, hdim = q.shape
    return pl.pallas_call(
        functools.partial(own_kernel, rows, group, factor),
        out_shape=[
            pltpu.VMEM((n, 2 * hdim), jnp.bfloat16),
            pltpu.VMEM((n, hdim), jnp.float32),
            pltpu.VMEM((n, 2 * hdim), jnp.float32),
        ],
        in_specs=[SMEM, SMEM, pl.BlockSpec(memory_space=pl.ANY), VMEM],
        out_specs=[VMEM] * 3,
        scratch_shapes=[
            pltpu.VMEM((n, hdim), jnp.bfloat16),
            pltpu.VMEM((rows, hdim), jnp.int32),
            pltpu.SemaphoreType.DMA(()),
        ],
        compiler_params=pltpu.CompilerParams(vmem_limit_bytes=28 << 20),
        cost_estimate=pl.CostEstimate(flops=1_500_000_000, bytes_accessed=1_500_000, transcendentals=1_500_000),
    )(me, doc_lengths, q, kv)


def later_stage(me, doc_lengths, state, blocks, origin, last, rows, factor):
    qx, m, la = state
    n, hdim = m.shape
    count = len(blocks)
    held = [pltpu.VMEM((n, hdim), jnp.float32), pltpu.VMEM((n, 2 * hdim), jnp.float32)]
    outs = [pltpu.VMEM((n, hdim), jnp.bfloat16)] if last else []
    result = pl.pallas_call(
        functools.partial(later_kernel, origin, count, last, rows, factor),
        out_shape=outs + held,
        in_specs=[SMEM, SMEM] + [VMEM] * (count + 3),
        out_specs=[VMEM] * (len(outs) + 2),
        input_output_aliases={3 + count + i: len(outs) + i for i in range(2)},
        scratch_shapes=[pltpu.VMEM((count, rows, 2 * hdim), jnp.bfloat16)] * 2,
        compiler_params=pltpu.CompilerParams(vmem_limit_bytes=28 << 20),
        cost_estimate=pl.CostEstimate(
            flops=2_000_000_000 * count, bytes_accessed=300_000 * count, transcendentals=2_000_000 * count
        ),
    )(me, doc_lengths, qx, *blocks, m, la)
    return result[0] if last else (qx, *result)


def on_device(queries, keys, values, doc_lengths):
    rows, group, hdim = queries.shape
    count = lax.axis_size("ctx")
    heads = lax.axis_size("head")
    factor = 1.4426950408889634 / hdim**0.5
    me = lax.axis_index("ctx").reshape(1)
    own = jnp.concatenate([keys[:, 0, :], values[:, 0, :]], axis=1)

    def swap(x, bit):
        return lax.ppermute(x, "ctx", [(i, i ^ bit) for i in range(count)])

    def plane(x):
        return lax.ppermute(x, "ctx", [(i, i + 4) for i in range(count - 4)])

    z1 = plane(own)
    x0 = swap(own, 2)
    c0 = swap(own, 1)
    state = own_stage(me, doc_lengths, queries.reshape(rows * group, hdim), own, rows, group, factor)
    z1, x0, c0, state = lax.optimization_barrier((z1, x0, c0, state))
    z2 = plane(z1)
    x1 = swap(z1, 2)
    xc0 = swap(x0, 1)
    c1 = swap(z1, 1)
    state = later_stage(me, doc_lengths, state, [c0, x0, xc0, z1, c1], 1, False, rows, factor)
    z2, x1, state = lax.optimization_barrier((z2, x1, state))
    x2 = lax.ppermute(z2, "ctx", [(i, i ^ 2) for i in range(count) if i & 2])
    xc1 = swap(x1, 1)
    c2 = swap(z2, 1)
    state = later_stage(me, doc_lengths, state, [x1, xc1, z2, c2], 6, False, rows, factor)
    x2, state = lax.optimization_barrier((x2, state))
    xc2 = swap(x2, 1)
    out = later_stage(me, doc_lengths, state, [x2, xc2], 10, True, rows, factor)
    out = lax.all_to_all(out.reshape(heads, -1, hdim), "head", split_axis=0, concat_axis=0, tiled=True)
    out = out.reshape(heads, rows // heads, group, hdim)
    return jnp.transpose(out, (1, 0, 2, 3)).reshape(rows // heads, heads * group * hdim)


def solution(mesh):
    placed = (P("ctx", "head", None), P("ctx", "head", None), P("ctx", "head", None), P())

    return jax.shard_map(
        on_device, mesh=mesh, in_specs=placed, out_specs=P(("ctx", "head"), None), check_vma=False
    )
```

time: 85.1 us -> 76.1 us (0.89)
  the two profiles are of different devices: /device:TPU:224 before, /device:TPU:192 now
where the time goes in v3:
time: 76.1 us; the launch traced here: 75.3 us
  Pallas kernels  32.3 us (42%)
  blocking collectives  21.3 us (28%)
  starting transfers between devices  14.8 us (19%)
  local copies, waits for them, and re-layouts  3.86 us (5%)
  waiting for transfers between devices  1.9 us (2%)
  other arithmetic  1 us (1%)
    pallas_call x3, Pallas kernels, later_stage(): pl.pallas_call(functools.partial(later_kernel, origin, count, last, rows,...  27.4 us
    all_to_all x1, blocking collectives, on_device(): lax.all_to_all(out.reshape(heads, -1, hdim), 'head', split_axis=0, concat...  21.3 us
    ppermute x8, starting transfers between devices, swap(): return lax.ppermute(x, 'ctx', [(i, i ^ bit) for i in range(count)])  7.68 us
    ppermute x2, starting transfers between devices, plane(): return lax.ppermute(x, 'ctx', [(i, i + 4) for i in range(count - 4)])  5.83 us
    pallas_call x1, Pallas kernels, own_stage(): pl.pallas_call(functools.partial(own_kernel, rows, group, factor), out_sh...  4.83 us
    unnamed x5, local copies, waits for them, and re-layouts  3.57 us
  transfers between devices with their start and end apart: 11, of which 3 were waited for; matrix products, arithmetic and copies ran while one was open for 0% of the time, Pallas kernels for 32%

profile of v3, /device:TPU:192, one launch (start us, length us, event | category | flops | bytes accessed | tf_op | source)
XLA Modules:
  0.0 75.3 jit_solution(1382155645943963439)
XLA Ops:
  0.0 1.0 %pad_maximum_fusion.kv_ref = bf16[512,256]{1,0:T(8,128)(2,1)S(1)} fusion(bf16[512,128]{1,0:T(8,128)(2,1)} %bitcast.16, bf16[512,128]{1,0:T(8,128)(2,1)} %bitcast.17), kind=kLoop, calls=%fused_computation.1 | loop fusion | flops 524288 | bytes 524288 | tf_op jit(solution)/shard_map/concatenate | solution.py:203
  1.0 0.1 collective-permute-start.2
  1.1 3.1 %collective-permute-start.1 = (bf16[512,256]{1,0:T(8,128)(2,1)S(1)}, bf16[512,256]{1,0:T(8,128)(2,1)S(1)}, u32[]{:S(2)}, u32[]{:S(2)}) collective-permute-start(bf16[512,256]{1,0:T(8,128)(2,1)S(1)} %pad_maximum_fusion.kv_ref), channel_id=1, source_target_pairs={{0,16},{8,24},{16,0},{24,8},{32,48},{40,56},{48,32},{56,40},{64,80... | collective-permute-start | bytes 786440 | tf_op jit(solution)/shard_map/ppermute | solution.py:206
  4.2 2.9 %collective-permute-start = (bf16[512,256]{1,0:T(8,128)(2,1)S(1)}, bf16[512,256]{1,0:T(8,128)(2,1)S(1)}, u32[]{:S(2)}, u32[]{:S(2)}) collective-permute-start(bf16[512,256]{1,0:T(8,128)(2,1)S(1)} %pad_maximum_fusion.kv_ref), channel_id=1, source_target_pairs={{0,32},{8,40},{16,48},{24,56},{32,64},{40,72},{48,80},{56,88},{64,... | collective-permute-start | bytes 786440 | tf_op jit(solution)/shard_map/ppermute | solution.py:209
  7.1 0.0 copy-start
  7.2 1.2 %copy-done = bf16[512,8,128]{2,1,0:T(8,128)(2,1)S(1)} copy-done((bf16[512,8,128]{2,1,0:T(8,128)(2,1)S(1)}, bf16[512,8,128]{2,1,0:T(8,128)(2,1)}, u32[]{:S(2)}) %copy-start) | copy-done | bytes 1048600
  8.4 0.7 copy-done.1
  9.0 4.8 %shard_map.46 = (bf16[4096,256]{1,0:T(8,128)(2,1)S(1)}, f32[4096,128]{1,0:T(8,128)S(1)}, f32[4096,256]{1,0:T(8,128)S(1)}) custom-call(s32[1]{0:T(128)} %bitcast.me_ref, s32[64]{0:T(128)S(1)} %copy-done.1, bf16[4096,128]{1,0:T(8,128)(2,1)S(1)} %bitcast.13, bf16[512,256]{1,0:T(8,128)(2,1)S(1)} %pad_maximum_fusion.kv_ref), custom_call_target="tpu_custom_call" | custom-call | flops 1500000000 | bytes 1500000 | tf_op jit(solution)/shard_map/pallas_call | solution.py:157
  13.9 0.0 collective-permute-done.2.refs_0_
  13.9 0.0 collective-permute-done.1.refs_1_
  13.9 0.6 collective-permute-done.refs_3_
  14.5 0.0 collective-permute-start.5
  14.5 0.5 collective-permute-start.6
  15.0 0.5 collective-permute-start.4
  15.5 2.9 %collective-permute-start.3 = (bf16[512,256]{1,0:T(8,128)(2,1)S(1)}, bf16[512,256]{1,0:T(8,128)(2,1)S(1)}, u32[]{:S(2)}, u32[]{:S(2)}) collective-permute-start(bf16[512,256]{1,0:T(8,128)(2,1)S(1)} %collective-permute-done.refs_3_), channel_id=1, source_target_pairs={{0,32},{8,40},{16,48},{24,56},{32,64},{40,72},{48,80},{56,88},{64,... | collective-permute-start | bytes 786440 | tf_op jit(solution)/shard_map/ppermute | solution.py:209
  18.4 0.0 collective-permute-done.5.refs_2_
  18.4 0.0 collective-permute-done.6.refs_4_
  18.4 7.9 %shard_map.47 = (f32[4096,128]{1,0:T(8,128)S(1)}, f32[4096,256]{1,0:T(8,128)S(1)}) custom-call(s32[1]{0:T(128)} %bitcast.me_ref, s32[64]{0:T(128)S(1)} %copy-done.1, bf16[4096,256]{1,0:T(8,128)(2,1)S(1)} %get-tuple-element.46.qx_ref, bf16[512,256]{1,0:T(8,128)(2,1)S(1)} %collective-permute-done.2.refs_0_, ...), custom_call_target="tpu_custom_call", output_to_operand_aliasing={{0}: (8, {}), {1}: (9, {})} | custom-call | flops 10000000000 | bytes 1500000 | tf_op jit(solution)/shard_map/pallas_call | solution.py:182
  26.3 0.0 collective-permute-done.4.refs_0_
  26.3 2.9 %collective-permute-start.8 = (bf16[512,256]{1,0:T(8,128)(2,1)S(1)}, bf16[512,256]{1,0:T(8,128)(2,1)S(1)}, u32[]{:S(2)}, u32[]{:S(2)}) collective-permute-start(bf16[512,256]{1,0:T(8,128)(2,1)S(1)} %collective-permute-done.4.refs_0_), channel_id=1, source_target_pairs={{0,8},{8,0},{16,24},{24,16},{32,40},{40,32},{48,56},{56,48},{64,72... | collective-permute-start | bytes 786440 | tf_op jit(solution)/shard_map/ppermute | solution.py:206
  29.2 0.1 collective-permute-start.9
  29.3 1.3 %collective-permute-start.7 = (bf16[512,256]{1,0:T(8,128)(2,1)S(1)}, bf16[512,256]{1,0:T(8,128)(2,1)S(1)}, u32[]{:S(2)}, u32[]{:S(2)}) collective-permute-start(bf16[512,256]{1,0:T(8,128)(2,1)S(1)} %collective-permute-done.3.refs_2_), channel_id=1, source_target_pairs={{16,0},{24,8},{48,32},{56,40},{80,64},{88,72},{112,96},{120,104},{... | collective-permute-start | bytes 786440 | tf_op jit(solution)/shard_map/ppermute | solution.py:222
  30.6 0.0 collective-permute-done.8.refs_1_
  30.6 0.1 collective-permute-done.9.refs_3_
  30.8 11.4 %shard_map.48 = (f32[4096,128]{1,0:T(8,128)S(1)}, f32[4096,256]{1,0:T(8,128)S(1)}) custom-call(s32[1]{0:T(128)} %bitcast.me_ref, s32[64]{0:T(128)S(1)} %copy-done.1, bf16[4096,256]{1,0:T(8,128)(2,1)S(1)} %get-tuple-element.46.qx_ref, bf16[512,256]{1,0:T(8,128)(2,1)S(1)} %collective-permute-done.4.refs_0_, ...), custom_call_target="tpu_custom_call", output_to_operand_aliasing={{0}: (7, {}), {1}: (8, {})} | custom-call | flops 8000000000 | bytes 1200000 | tf_op jit(solution)/shard_map/pallas_call | solution.py:182
  42.2 0.0 collective-permute-done.7.refs_0_
  42.2 0.5 collective-permute-start.10
  42.7 1.2 %collective-permute-done.10.refs_1_ = bf16[512,256]{1,0:T(8,128)(2,1)S(1)} collective-permute-done((bf16[512,256]{1,0:T(8,128)(2,1)S(1)}, bf16[512,256]{1,0:T(8,128)(2,1)S(1)}, u32[]{:S(2)}, u32[]{:S(2)}) %collective-permute-start.10) | collective-permute-done | bytes 262176 | tf_op jit(solution)/shard_map/ppermute | solution.py:206
  43.8 8.1 %shard_map.49 = (bf16[4096,128]{1,0:T(8,128)(2,1)S(1)}, f32[4096,128]{1,0:T(8,128)S(1)}, f32[4096,256]{1,0:T(8,128)S(1)}) custom-call(s32[1]{0:T(128)} %bitcast.me_ref, s32[64]{0:T(128)S(1)} %copy-done.1, bf16[4096,256]{1,0:T(8,128)(2,1)S(1)} %get-tuple-element.46.qx_ref, ...), custom_call_target="tpu_custom_call", output_to_operand_aliasing={{1}: (5, {}), {2}: (6, {})} | custom-call | flops 4000000000 | bytes 600000 | tf_op jit(solution)/shard_map/pallas_call | solution.py:182
  52.0 21.3 %all_to_all.5 = bf16[8,512,128]{2,1,0:T(8,128)(2,1)S(1)} all-to-all(bf16[8,512,128]{2,1,0:T(8,128)(2,1)S(1)} %bitcast.12), channel_id=1, replica_groups=mesh['ctx'=32,'head'=8] {'head'}, dimensions={0} | all-to-all | bytes 2097152 | tf_op jit(solution)/shard_map/all_to_all | solution.py:229
  73.3 0.3 copy.11
  73.6 1.7 %copy.14 = bf16[8,8,64,128]{3,1,2,0:T(8,128)(2,1)} copy(bf16[8,8,64,128]{3,2,1,0:T(8,128)(2,1)S(1)} %bitcast.15) | data formatting | bytes 2097152
  (2 shorter events, 0.0 us)
Async XLA Ops:
  1.0 12.9 %collective-permute-start.2 = (bf16[512,256]{1,0:T(8,128)(2,1)S(1)}, bf16[512,256]{1,0:T(8,128)(2,1)S(1)}, u32[]{:S(2)}, u32[]{:S(2)}) collective-permute-start(bf16[512,256]{1,0:T(8,128)(2,1)S(1)} %pad_maximum_fusion.kv_ref), channel_id=1, source_target_pairs={{0,8},{8,0},{16,24},{24,16},{32,40},{40,32},{48,56},{56,48},{64,72... | collective-permute-start | bytes 786440 | tf_op jit(solution)/shard_map/ppermute | solution.py:206
  1.1 12.8 %collective-permute-start.1 = (bf16[512,256]{1,0:T(8,128)(2,1)S(1)}, bf16[512,256]{1,0:T(8,128)(2,1)S(1)}, u32[]{:S(2)}, u32[]{:S(2)}) collective-permute-start(bf16[512,256]{1,0:T(8,128)(2,1)S(1)} %pad_maximum_fusion.kv_ref), channel_id=1, source_target_pairs={{0,16},{8,24},{16,0},{24,8},{32,48},{40,56},{48,32},{56,40},{64,80... | collective-permute-start | bytes 786440 | tf_op jit(solution)/shard_map/ppermute | solution.py:206
  4.2 10.2 %collective-permute-start = (bf16[512,256]{1,0:T(8,128)(2,1)S(1)}, bf16[512,256]{1,0:T(8,128)(2,1)S(1)}, u32[]{:S(2)}, u32[]{:S(2)}) collective-permute-start(bf16[512,256]{1,0:T(8,128)(2,1)S(1)} %pad_maximum_fusion.kv_ref), channel_id=1, source_target_pairs={{0,32},{8,40},{16,48},{24,56},{32,64},{40,72},{48,80},{56,88},{64,... | collective-permute-start | bytes 786440 | tf_op jit(solution)/shard_map/ppermute | solution.py:209
  7.1 1.2 %copy-start = (bf16[512,8,128]{2,1,0:T(8,128)(2,1)S(1)}, bf16[512,8,128]{2,1,0:T(8,128)(2,1)}, u32[]{:S(2)}) copy-start(bf16[512,8,128]{2,1,0:T(8,128)(2,1)} %param.4) | copy-start | bytes 3145732
  8.4 0.7 copy-start.1
  14.5 3.9 %collective-permute-start.5 = (bf16[512,256]{1,0:T(8,128)(2,1)S(1)}, bf16[512,256]{1,0:T(8,128)(2,1)S(1)}, u32[]{:S(2)}, u32[]{:S(2)}) collective-permute-start(bf16[512,256]{1,0:T(8,128)(2,1)S(1)} %collective-permute-done.1.refs_1_), channel_id=1, source_target_pairs={{0,8},{8,0},{16,24},{24,16},{32,40},{40,32},{48,56},{56,48},{64,72... | collective-permute-start | bytes 786440 | tf_op jit(solution)/shard_map/ppermute | solution.py:206
  14.5 3.9 %collective-permute-start.6 = (bf16[512,256]{1,0:T(8,128)(2,1)S(1)}, bf16[512,256]{1,0:T(8,128)(2,1)S(1)}, u32[]{:S(2)}, u32[]{:S(2)}) collective-permute-start(bf16[512,256]{1,0:T(8,128)(2,1)S(1)} %collective-permute-done.refs_3_), channel_id=1, source_target_pairs={{0,8},{8,0},{16,24},{24,16},{32,40},{40,32},{48,56},{56,48},{64,72... | collective-permute-start | bytes 786440 | tf_op jit(solution)/shard_map/ppermute | solution.py:206
  15.0 11.4 %collective-permute-start.4 = (bf16[512,256]{1,0:T(8,128)(2,1)S(1)}, bf16[512,256]{1,0:T(8,128)(2,1)S(1)}, u32[]{:S(2)}, u32[]{:S(2)}) collective-permute-start(bf16[512,256]{1,0:T(8,128)(2,1)S(1)} %collective-permute-done.refs_3_), channel_id=1, source_target_pairs={{0,16},{8,24},{16,0},{24,8},{32,48},{40,56},{48,32},{56,40},{64,80... | collective-permute-start | bytes 786440 | tf_op jit(solution)/shard_map/ppermute | solution.py:206
  15.5 10.9 %collective-permute-start.3 = (bf16[512,256]{1,0:T(8,128)(2,1)S(1)}, bf16[512,256]{1,0:T(8,128)(2,1)S(1)}, u32[]{:S(2)}, u32[]{:S(2)}) collective-permute-start(bf16[512,256]{1,0:T(8,128)(2,1)S(1)} %collective-permute-done.refs_3_), channel_id=1, source_target_pairs={{0,32},{8,40},{16,48},{24,56},{32,64},{40,72},{48,80},{56,88},{64,... | collective-permute-start | bytes 786440 | tf_op jit(solution)/shard_map/ppermute | solution.py:209
  26.3 4.3 %collective-permute-start.8 = (bf16[512,256]{1,0:T(8,128)(2,1)S(1)}, bf16[512,256]{1,0:T(8,128)(2,1)S(1)}, u32[]{:S(2)}, u32[]{:S(2)}) collective-permute-start(bf16[512,256]{1,0:T(8,128)(2,1)S(1)} %collective-permute-done.4.refs_0_), channel_id=1, source_target_pairs={{0,8},{8,0},{16,24},{24,16},{32,40},{40,32},{48,56},{56,48},{64,72... | collective-permute-start | bytes 786440 | tf_op jit(solution)/shard_map/ppermute | solution.py:206
  29.2 1.5 %collective-permute-start.9 = (bf16[512,256]{1,0:T(8,128)(2,1)S(1)}, bf16[512,256]{1,0:T(8,128)(2,1)S(1)}, u32[]{:S(2)}, u32[]{:S(2)}) collective-permute-start(bf16[512,256]{1,0:T(8,128)(2,1)S(1)} %collective-permute-done.3.refs_2_), channel_id=1, source_target_pairs={{0,8},{8,0},{16,24},{24,16},{32,40},{40,32},{48,56},{56,48},{64,72... | collective-permute-start | bytes 786440 | tf_op jit(solution)/shard_map/ppermute | solution.py:206
  29.3 12.9 %collective-permute-start.7 = (bf16[512,256]{1,0:T(8,128)(2,1)S(1)}, bf16[512,256]{1,0:T(8,128)(2,1)S(1)}, u32[]{:S(2)}, u32[]{:S(2)}) collective-permute-start(bf16[512,256]{1,0:T(8,128)(2,1)S(1)} %collective-permute-done.3.refs_2_), channel_id=1, source_target_pairs={{16,0},{24,8},{48,32},{56,40},{80,64},{88,72},{112,96},{120,104},{... | collective-permute-start | bytes 786440 | tf_op jit(solution)/shard_map/ppermute | solution.py:222
  42.2 1.6 %collective-permute-start.10 = (bf16[512,256]{1,0:T(8,128)(2,1)S(1)}, bf16[512,256]{1,0:T(8,128)(2,1)S(1)}, u32[]{:S(2)}, u32[]{:S(2)}) collective-permute-start(bf16[512,256]{1,0:T(8,128)(2,1)S(1)} %collective-permute-done.7.refs_0_), channel_id=1, source_target_pairs={{0,8},{8,0},{16,24},{24,16},{32,40},{40,32},{48,56},{56,48},{64,72... | collective-permute-start | bytes 786440 | tf_op jit(solution)/shard_map/ppermute | solution.py:206
